TPU v7x, 32 devices: a whole 2x2x4 slice. The times are simulated.
32 devices in a mesh: blk: 8 (over z, y), tm: 4 (over x, core).
Axes of the slice: x: 2, y: 2, z: 4, core: 2. Of those that a mesh axis runs over, the one named last changes fastest.
Arguments:
- solution: float32 [512, 128, 1024], P('blk', 'tm'), may hold values from -6 to 6
- residual: float32 [512, 128, 1024], P('blk', 'tm'), may hold values from -12 to 12
- direction: float32 [512, 128, 1024], P('blk', 'tm'), may hold values from -6 to 6
- noise_var: float32 [512, 128, 1024], P('blk', 'tm'), may hold values from 0.5 to 2
- legendre: bfloat16 [512, 512, 512], P('blk', 'tm'), may hold values from -0.25 to 0.25
- temporal: float32 [512, 128, 128], P('tm'), may hold values from -3 to 3.5, as said below
- order_table: int32 [512], replicated, may hold values from 0 to 511, as said below
Outputs:
- solution_new: float32 [512, 128, 1024], P('blk', 'tm')
- residual_new: float32 [512, 128, 1024], P('blk', 'tm')
- direction_new: float32 [512, 128, 1024], P('blk', 'tm')
Inputs may be any that keep to these rules, and one draw needn't show every extreme that they name: `order_table`: each value 0 to 511 appears once. In each aligned block of 64 entries, entry 32 + k equals 511 minus entry k, so each block holds pairs of orders m and 511 - m. `temporal`: each matrix is symmetric and positive definite.
All inputs are finite; a program needn't handle non-finite values.
Results may differ from a plain program's by a relative error of at most 0.0048.
Values may be sent and summed in bfloat16 or wider, within the bound.
No kernel may reach another device: no remote copies, remote signals or barrier semaphores. Data moves between devices by JAX's collectives and lax.ppermute only.
A program may use at most 192 MiB of HBM per device.

v0:
```python
import math

import jax
import jax.numpy as jnp
from jax import lax
from jax.experimental import pallas as pl
from jax.experimental.pallas import tpu as pltpu
from jax.sharding import Mesh, PartitionSpec as P


LANES = 128
PACK = 16
CHUNKS = 4
BF = jnp.bfloat16
F32 = jnp.float32


def trig_table(orders, length):
    points = jnp.arange(length, dtype=jnp.int32)
    phases = points[:, None] * orders[None, :] % length
    angles = phases.astype(jnp.float32) * (2.0 * math.pi / length)
    scaling_factor = 1.0 / math.sqrt(length / 2.0)
    stacked = jnp.stack([jnp.cos(angles), jnp.sin(angles)], axis=-1) * scaling_factor
    return stacked.reshape(length, 2 * orders.shape[0])


def plain_body(solution, residual, direction, noise_var, legendre, temporal, order_table):
    per_device, deg_dev, lat_all = legendre.shape
    latitude_rows_local, time_dev, longitude = direction.shape
    highest = lax.Precision.HIGHEST
    blk, tm = ("blk",), ("x", "core")
    lookup_table = trig_table(order_table, longitude)
    own_orders = lax.dynamic_slice_in_dim(order_table, lax.axis_index(blk) * per_device, per_device)
    own_degrees = lax.axis_index(tm) * deg_dev + jnp.arange(deg_dev, dtype=jnp.int32)
    keep_mask = own_degrees[None, :, None] >= own_orders[:, None, None]
    mask_applied = jnp.where(keep_mask, legendre, jnp.zeros_like(legendre))
    spectra = jnp.einsum("atj,jc->act", direction, lookup_table, precision=highest).astype(BF)
    cycles = lax.all_to_all(
        spectra.reshape(latitude_rows_local, -1), blk, split_axis=1, concat_axis=0, tiled=True
    )
    cycles = cycles.reshape(lat_all, per_device, 2, time_dev)
    full_table = lax.all_gather(mask_applied, tm, axis=1, tiled=True)
    coeffs = jnp.einsum("kla,akct->kclt", full_table, cycles, preferred_element_type=F32)
    coeffs = lax.all_to_all(coeffs, tm, split_axis=2, concat_axis=3, tiled=True)
    mixed = jnp.einsum("ltu,kclu->kclt", temporal, coeffs, precision=highest).astype(BF)
    returned = lax.all_to_all(mixed, tm, split_axis=3, concat_axis=2, tiled=True)
    terms = jnp.einsum("kla,kclt->takc", full_table, returned, preferred_element_type=F32)
    terms = terms.reshape(time_dev, lat_all, per_device * 2)
    column_entries = lax.all_to_all(terms, blk, split_axis=1, concat_axis=2, tiled=True)
    harmonic_synthesis = jnp.einsum("qpo,lo->pql", column_entries, lookup_table, precision=highest)
    product = harmonic_synthesis + noise_var * direction
    every = blk + tm
    norm_now = lax.psum(jnp.sum(residual * residual), every)
    curvature = lax.psum(jnp.sum(direction * product), every)
    step_size = norm_now / curvature
    solution_new = solution + step_size * direction
    residual_new = residual - step_size * product
    norm_next = lax.psum(jnp.sum(residual_new * residual_new), every)
    direction_new = residual_new + norm_next / norm_now * direction
    return (solution_new, residual_new, direction_new)


def swap_halves(v):
    half = LANES // 2
    return jnp.concatenate([v[..., half:], v[..., :half]], axis=-1)


def low_half(shape):
    return lax.broadcasted_iota(jnp.int32, shape, len(shape) - 1) < LANES // 2


def analysis_call(direction4, tables):
    cycles, lo_n, hi_n, length = direction4.shape
    cols = tables[0].shape[0]
    n_tab = len(tables)
    sub = 8
    steps = hi_n // sub
    parts_n = length // LANES

    def kernel(*refs):
        x_refs = refs[:parts_n]
        tab_refs = refs[parts_n : parts_n + n_tab]
        o_refs = refs[parts_n + n_tab : parts_n + 2 * n_tab]
        s_ref = refs[-1]
        h = pl.program_id(0)
        flat = [ref.reshape(cycles * lo_n * sub, LANES) for ref in x_refs]

        def pair(i, carry):
            parts = []
            for ii in range(2):
                for lo in range(lo_n):
                    at = pl.ds(lo * sub + 2 * i + ii, cycles, stride=lo_n * sub)
                    parts.append(jnp.concatenate([ref[at, :].astype(BF) for ref in flat], axis=1))
            x = jnp.concatenate(parts, axis=0)
            for n in range(n_tab):
                y = lax.dot_general(
                    tab_refs[n][...], x, (((1,), (1,)), ((), ())), preferred_element_type=F32
                )
                for ii in range(2):
                    s_ref[n, pl.ds(h * sub + 2 * i + ii, cols, stride=hi_n), :] = y[
                        :, ii * LANES : (ii + 1) * LANES
                    ]
            return carry

        lax.fori_loop(0, sub // 2, pair, 0)

        @pl.when(h == steps - 1)
        def _():
            for n in range(n_tab):
                o_refs[n][...] = s_ref[n].reshape(cols, hi_n, LANES).astype(BF)

    out = jax.ShapeDtypeStruct((cols, hi_n, LANES), BF)
    return pl.pallas_call(
        kernel,
        out_shape=(out,) * n_tab,
        grid=(steps,),
        in_specs=[
            pl.BlockSpec((cycles, lo_n, sub, LANES), lambda h, p=p: (0, 0, h, p))
            for p in range(parts_n)
        ]
        + [pl.BlockSpec((cols, length), lambda h: (0, 0))] * n_tab,
        out_specs=(pl.BlockSpec((cols, hi_n, LANES), lambda h: (0, 0, 0)),) * n_tab,
        scratch_shapes=[pltpu.VMEM((n_tab, cols * hi_n, LANES), F32)],
        compiler_params=pltpu.CompilerParams(vmem_limit_bytes=60 << 20),
        cost_estimate=pl.CostEstimate(
            flops=2 * n_tab * cols * cycles * lo_n * hi_n * length,
            bytes_accessed=direction4.size * 4 + n_tab * cols * length * 2,
            transcendentals=0,
        ),
        name="analysis",
    )(*[direction4] * parts_n, *tables)


def degree_call(scalars, legendre, temporal, gathered, chunk, n_x):
    _, deg_dev, lat_all = legendre.shape
    time_all = temporal.shape[-1]
    n_pieces = len(gathered)
    nb, _, chunk_n, hi_n, _ = gathered[0].shape
    time_dev = 2 * hi_n
    kb = 4
    lb = 16
    n1 = chunk_n // kb
    n2 = deg_dev // lb
    pitch = deg_dev + 8
    rows = 2 * time_all
    first = chunk * n1

    def kernel(sc_ref, leg_ref, tmp_ref, *refs):
        r_refs = refs[:n_pieces]
        keep_ref, send_ref, c_ref, r_scr, g_scr = refs[n_pieces:]
        step = pl.program_id(0)
        low = low_half((hi_n, LANES))

        def masked(kk, k):
            order = sc_ref[1 + 2 * n_pieces + k]
            degree = sc_ref[0] + lax.broadcasted_iota(jnp.int32, (deg_dev, lat_all), 0)
            values = leg_ref[kk]
            return jnp.where(degree >= order, values, jnp.zeros_like(values))

        @pl.when(step < n1)
        def _():
            for kk in range(kb):
                for q in range(n_pieces):
                    base = sc_ref[1 + q] * time_dev
                    for c in range(2):
                        for p in range(nb // 2):
                            even = r_refs[q][2 * p, c, kk]
                            odd = r_refs[q][2 * p + 1, c, kk]
                            for lo in range(2):
                                at = pl.multiple_of(c * time_all + base + lo * hi_n, hi_n)
                                if lo == 0:
                                    v = jnp.where(low, even, swap_halves(odd))
                                else:
                                    v = jnp.where(low, swap_halves(even), odd)
                                r_scr[kk, pl.ds(at, hi_n), p * LANES : (p + 1) * LANES] = v
                k = step * kb + kk
                y = lax.dot_general(
                    masked(kk, k), r_scr[kk], (((1,), (1,)), ((), ())), preferred_element_type=F32
                )
                for c in range(2):
                    at = pl.multiple_of((k * 2 + c) * pitch, 8)
                    c_ref[pl.ds(at, deg_dev), :] = y[:, c * time_all : (c + 1) * time_all]

        @pl.when((step >= n1) & (step < n1 + n2))
        def _():
            for i in range(lb):
                at = (step - n1) * lb + i
                v = c_ref[pl.ds(at, 2 * chunk_n, stride=pitch), :].astype(BF)
                w = tmp_ref[i]
                c_ref[pl.ds(at, 2 * chunk_n, stride=pitch), :] = jnp.dot(
                    v, w, preferred_element_type=F32
                )

        @pl.when(step >= n1 + n2)
        def _():
            for kk in range(kb):
                k = (step - n1 - n2) * kb + kk
                m = masked(kk, k)
                for c in range(2):
                    at = pl.multiple_of((k * 2 + c) * pitch, 8)
                    v = c_ref[pl.ds(at, deg_dev), :].astype(BF)
                    g_scr[kk, c * time_all : (c + 1) * time_all, :] = lax.dot_general(
                        v, m, (((0,), (0,)), ((), ())), preferred_element_type=F32
                    ).astype(BF)
                for q in range(n_pieces):
                    base = sc_ref[1 + n_pieces + q] * time_dev
                    out = keep_ref if q < n_x else send_ref
                    for c in range(2):
                        for p in range(nb // 2):
                            at = pl.multiple_of(c * time_all + base, hi_n)
                            lanes = slice(p * LANES, (p + 1) * LANES)
                            v0 = g_scr[kk, pl.ds(at, hi_n), lanes]
                            v1 = g_scr[kk, pl.ds(at + hi_n, hi_n), lanes]
                            out[q % n_x, 2 * p, c, kk] = jnp.where(low, v0, swap_halves(v1))
                            out[q % n_x, 2 * p + 1, c, kk] = jnp.where(low, swap_halves(v0), v1)

    def leg_map(s, sc):
        return (
            first + jnp.where(s < n1, s, jnp.where(s < n1 + n2, n1 - 1, s - n1 - n2)),
            0,
            0,
        )

    piece = (nb, 2, chunk_n, hi_n, LANES)
    out_block = pl.BlockSpec(
        (n_x, nb, 2, kb, hi_n, LANES),
        lambda s, sc: (0, 0, 0, jnp.maximum(s - n1 - n2, 0), 0, 0),
    )
    out_shape = jax.ShapeDtypeStruct((n_x,) + piece, BF)
    flops = 4 * chunk_n * deg_dev * lat_all * rows + 2 * deg_dev * 2 * chunk_n * time_all**2
    return pl.pallas_call(
        kernel,
        out_shape=(out_shape, out_shape),
        grid_spec=pltpu.PrefetchScalarGridSpec(
            num_scalar_prefetch=1,
            grid=(n1 + n2 + n1,),
            in_specs=[
                pl.BlockSpec((kb, deg_dev, lat_all), leg_map),
                pl.BlockSpec(
                    (lb, time_all, time_all),
                    lambda s, sc: (jnp.clip(s - n1, 0, n2 - 1), 0, 0),
                ),
            ]
            + [
                pl.BlockSpec(
                    (nb, 2, kb, hi_n, LANES),
                    lambda s, sc: (0, 0, jnp.minimum(s, n1 - 1), 0, 0),
                )
            ]
            * n_pieces,
            out_specs=(out_block, out_block),
            scratch_shapes=[
                pltpu.VMEM((2 * chunk_n * pitch, time_all), F32),
                pltpu.VMEM((kb, rows, lat_all), BF),
                pltpu.VMEM((kb, rows, lat_all), BF),
            ],
        ),
        compiler_params=pltpu.CompilerParams(vmem_limit_bytes=60 << 20),
        cost_estimate=pl.CostEstimate(
            flops=flops,
            bytes_accessed=4 * chunk_n * deg_dev * lat_all
            + temporal.size * 2
            + 4 * n_pieces * gathered[0].size,
            transcendentals=0,
        ),
        name="degrees",
    )(scalars, legendre, temporal, *gathered)


def synthesis_call(received, tables, previous, fields, scale):
    n_tab = len(received)
    cols, hi_n, _ = received[0].shape
    length = tables[0].shape[-1]
    lo_n = 2
    cycles = LANES // lo_n
    sub = 8
    jb = 512
    last = previous is not None
    n_grid = 3 if last else 2

    def kernel(*refs):
        rec_refs = refs[:n_tab]
        tab_refs = refs[n_tab : 2 * n_tab]
        grid_refs = refs[2 * n_tab : 2 * n_tab + n_grid]
        o_ref = refs[2 * n_tab + n_grid]
        sum_ref = refs[2 * n_tab + n_grid + 1] if last else None
        s_ref = refs[-1]
        h, j = pl.program_id(0), pl.program_id(1)
        if last:
            p_ref = o_ref.at[h, j]
            d_ref, r_ref = (refs[2 * n_tab + n_grid + n].at[h, j] for n in (2, 3))
        else:
            p_ref = refs[-2]

        @pl.when((h == 0) & (j == 0))
        def _():
            for n in range(n_tab):
                s_ref[n * cols * hi_n : (n + 1) * cols * hi_n, :] = (
                    rec_refs[n][...].astype(F32).reshape(cols * hi_n, LANES)
                )
            if last:
                sum_ref[...] = jnp.zeros_like(sum_ref)

        def one(i, carry):
            y = None
            for n in range(n_tab):
                at = pl.ds(n * cols * hi_n + h * sub + i, cols, stride=hi_n)
                v = s_ref[at, :].astype(BF)
                term = lax.dot_general(
                    v, tab_refs[n][...], (((0,), (0,)), ((), ())), preferred_element_type=F32
                )
                y = term if y is None else y + term
            y = y * scale
            for lo in range(lo_n):
                for part in range(jb // LANES):
                    p_ref[part, pl.ds(lo * sub + i, cycles, stride=lo_n * sub), :] = y[
                        lo * cycles : (lo + 1) * cycles, part * LANES : (part + 1) * LANES
                    ]
            return carry

        lax.fori_loop(0, sub, one, 0)
        group = 8

        def finish(i, carry):
            carry = list(carry)
            block = pl.ds(i * group, group)
            for part in range(jb // LANES):
                lanes = slice(part * LANES, (part + 1) * LANES)
                span = group * lo_n * sub
                rows = pl.ds(pl.multiple_of(i * span, span), span)
                p = p_ref[part, rows, :].reshape(group, lo_n, sub, LANES)
                if last:
                    p = p + grid_refs[0][block, :, :, lanes]
                    d = grid_refs[1][block, :, :, lanes]
                    r = grid_refs[2][block, :, :, lanes]
                    for n, term in enumerate((r * r, d * p, r * p, p * p)):
                        carry[n] = carry[n] + jnp.sum(term, axis=(0, 1))
                    for ref, v in ((p_ref, p), (d_ref, d), (r_ref, r)):
                        ref[part, rows, :] = v.reshape(span, LANES)
                else:
                    p = p + grid_refs[0][block, :, :, lanes] * grid_refs[1][block, :, :, lanes]
                    o_ref[block, :, :, lanes] = p
            return tuple(carry)

        zero = (jnp.zeros((sub, LANES), F32),) * 4
        sums = lax.fori_loop(0, cycles // group, finish, zero)
        if last:
            for n in range(4):
                sum_ref[n : n + 1, :] = sum_ref[n : n + 1, :] + jnp.sum(
                    sums[n], axis=0, keepdims=True
                )

    grid_block = pl.BlockSpec((cycles, lo_n, sub, jb), lambda h, j: (0, 0, h, j))
    in_specs = (
        [pl.BlockSpec((cols, hi_n, LANES), lambda h, j: (0, 0, 0))] * n_tab
        + [pl.BlockSpec((cols, jb), lambda h, j: (0, j))] * n_tab
        + [grid_block] * n_grid
    )
    tile_rows = cycles * lo_n * sub
    if last:
        held = pltpu.VMEM((hi_n // sub, length // jb, jb // LANES, tile_rows, LANES), F32)
        whole = pl.BlockSpec(memory_space=pltpu.VMEM)
        out_shape = [held, jax.ShapeDtypeStruct((sub, LANES), F32), held, held]
        out_specs = [whole, pl.BlockSpec((sub, LANES), lambda h, j: (0, 0)), whole, whole]
    else:
        out_shape = [jax.ShapeDtypeStruct((cycles, lo_n, hi_n, length), F32)]
        out_specs = [grid_block]
    grids = ((previous,) if last else ()) + tuple(fields)
    return pl.pallas_call(
        kernel,
        out_shape=tuple(out_shape),
        grid=(hi_n // sub, length // jb),
        in_specs=in_specs,
        out_specs=tuple(out_specs),
        scratch_shapes=([] if last else [pltpu.VMEM((jb // LANES, tile_rows, LANES), F32)])
        + [pltpu.VMEM((n_tab * cols * hi_n, LANES), F32)],
        compiler_params=pltpu.CompilerParams(vmem_limit_bytes=(24 << 20) if last else (60 << 20)),
        cost_estimate=pl.CostEstimate(
            flops=2 * n_tab * cols * LANES * hi_n * length,
            bytes_accessed=4 * cycles * lo_n * hi_n * length * (n_grid + 1),
            transcendentals=0,
        ),
        name="synthesis",
    )(*received, *tables, *grids)


def update_call(sums, solution4, held):
    cycles, lo_n, hi_n, length = solution4.shape
    _, steps_j, parts, _, _ = held[0].shape
    sub, jb = hi_n // held[0].shape[0], length // steps_j
    group = 8
    span = group * lo_n * sub

    n_sums = len(sums)

    def kernel(*refs):
        x_ref, p_ref, r_ref, d_ref, xo_ref, ro_ref, do_ref = refs[n_sums:]
        h, j = pl.program_id(0), pl.program_id(1)
        total = refs[0][...]
        for ref in refs[1:n_sums]:
            total = total + ref[...]
        norm_now, curvature, cross, square = (
            jnp.sum(total[n : n + 1], keepdims=True) for n in range(4)
        )
        step = norm_now / curvature
        norm_next = norm_now - 2.0 * (step * cross) + step * (step * square)
        ratio = norm_next / norm_now

        def some(i, carry):
            block = pl.ds(i * group, group)
            rows = pl.ds(pl.multiple_of(i * span, span), span)
            for part in range(parts):
                lanes = slice(part * LANES, (part + 1) * LANES)
                p, r, d = (
                    ref[h, j, part, rows, :].reshape(group, lo_n, sub, LANES)
                    for ref in (p_ref, r_ref, d_ref)
                )
                xo_ref[block, :, :, lanes] = x_ref[block, :, :, lanes] + step * d
                r = r - step * p
                ro_ref[block, :, :, lanes] = r
                do_ref[block, :, :, lanes] = r + ratio * d
            return carry

        lax.fori_loop(0, cycles // group, some, 0)

    spec = pl.BlockSpec((cycles, lo_n, sub, jb), lambda h, j: (0, 0, h, j))
    size = solution4.size
    return pl.pallas_call(
        kernel,
        out_shape=(jax.ShapeDtypeStruct(solution4.shape, F32),) * 3,
        grid=(hi_n // sub, steps_j),
        in_specs=[pl.BlockSpec(sums[0].shape, lambda h, j: (0, 0))] * n_sums
        + [spec]
        + [pl.BlockSpec(memory_space=pltpu.VMEM)] * 3,
        out_specs=(spec,) * 3,
        compiler_params=pltpu.CompilerParams(vmem_limit_bytes=24 << 20),
        cost_estimate=pl.CostEstimate(
            flops=6 * size, bytes_accessed=16 * size, transcendentals=0
        ),
        name="update",
    )(*sums, solution4, *(pltpu.with_memory_space_constraint(v, pltpu.VMEM) for v in held))


def add_call(values):
    def kernel(*refs):
        total = refs[0][...]
        for ref in refs[1:-1]:
            total = total + ref[...]
        refs[-1][...] = total

    return pl.pallas_call(
        kernel,
        out_shape=jax.ShapeDtypeStruct(values[0].shape, F32),
        compiler_params=pltpu.CompilerParams(vmem_limit_bytes=1 << 20),
        name="add",
    )(*values)


def sum_parts(values, n_blk, n_x, n_core):
    def stage(v, axes, perms):
        return [v] + [lax.ppermute(v, axes, perm) for perm in perms]

    n_tm = n_x * n_core
    tm = [[(i, (i + s) % n_tm) for i in range(n_tm)] for s in range(1, n_tm)]
    pair = [[(i, i ^ 1) for i in range(n_blk)]]
    rest = [[(i, (i + s) % n_blk) for i in range(n_blk)] for s in range(2, n_blk, 2)]
    values = add_call(stage(values, ("x", "core"), tm))
    values = add_call(stage(values, "blk", pair))
    return stage(values, "blk", rest)


def sine_table(phases, length):
    folded = jnp.abs(phases - length // 2) - length // 4
    x = folded.astype(F32) * (2.0 * math.pi / length)
    z = x * x
    value = jnp.full_like(z, -1.0 / math.factorial(11))
    for n in (9, 7, 5, 3, 1):
        value = value * z + (1.0 if n % 4 == 1 else -1.0) / math.factorial(n)
    return value * x


def fast_body(mesh, solution, residual, direction, noise_var, legendre, temporal, order_table):
    per_device, deg_dev, _ = legendre.shape
    cycles, time_dev, longitude = direction.shape
    nb, n_x, n_core = (mesh.shape[name] for name in ("blk", "x", "core"))
    lo_n = LANES // cycles
    hi_n = time_dev // lo_n
    chunk_n = per_device // CHUNKS
    cols = nb * 2 * chunk_n
    blk_i, x_i, core_i = (lax.axis_index(name) for name in ("blk", "x", "core"))
    grouped = order_table.reshape(nb, per_device)
    own_orders = lax.dynamic_slice_in_dim(order_table, blk_i * per_device, per_device)
    shape4 = (cycles, lo_n, hi_n, longitude)
    direction4, noise4, residual4 = (v.reshape(shape4) for v in (direction, noise_var, residual))
    quarter = (longitude // 4) * 3

    def table_of(chunk):
        orders = grouped[:, chunk * chunk_n : (chunk + 1) * chunk_n]
        points = jnp.arange(longitude, dtype=jnp.int32)
        turn = jnp.arange(2, dtype=jnp.int32) * quarter
        phases = orders[:, None, :, None] * points + turn[None, :, None, None]
        return sine_table(phases % longitude, longitude).astype(BF).reshape(cols, longitude)

    forth = [jnp.mod(x_i - s, n_x) * n_core + (core_i + o) % n_core for o in range(2) for s in range(n_x)]
    back = [jnp.mod(x_i + s, n_x) * n_core + (core_i + o) % n_core for o in range(2) for s in range(n_x)]
    base = (x_i * n_core + core_i) * deg_dev
    header = jnp.stack([base] + forth + back).astype(jnp.int32)
    swap = [(i, (i + 1) % n_core) for i in range(n_core)]

    def shift(v, s):
        return lax.ppermute(v, "x", [(i, (i + s) % n_x) for i in range(n_x)])

    def across(v):
        return lax.all_to_all(v, "blk", split_axis=0, concat_axis=0, tiled=True)

    tables = [table_of(0)]
    spectra = list(analysis_call(direction4, tables))
    piece = (nb, 2, chunk_n, hi_n, LANES)
    tables += [table_of(g) for g in range(1, CHUNKS)]
    spectra += list(analysis_call(direction4, tables[1:]))
    temporal_narrow = temporal.astype(BF)
    received = []
    for g in range(CHUNKS):
        mine = across(spectra[g].reshape(piece))
        own = [mine] + [shift(mine, s) for s in range(1, n_x)]
        pieces = own + [lax.ppermute(v, "core", swap) for v in own]
        scalars = jnp.concatenate([header, own_orders[g * chunk_n : (g + 1) * chunk_n]])
        keep, send = degree_call(scalars, legendre, temporal_narrow, pieces, g, n_x)
        other = lax.ppermute(send, "core", swap)
        halves = [keep[s].astype(F32) + other[s].astype(F32) for s in range(n_x)]
        halves = [halves[0].astype(BF)] + [v.astype(BF) for v in halves[1:]]
        parts = [shift(halves[s], s) for s in range(1, n_x)]
        total = halves[0].astype(F32)
        for part in parts:
            total = total + part.astype(F32)
        total = total.astype(BF)
        received.append(across(total).reshape(cols, hi_n, LANES))
    scale = 2.0 / longitude
    (partial,) = synthesis_call(received[:-1], tables[:-1], None, (noise4, direction4), scale)
    product, sums, near_d, near_r = synthesis_call(
        received[-1:], tables[-1:], partial, (direction4, residual4), scale
    )
    sums = sum_parts(sums, nb, n_x, n_core)
    out = update_call(sums, solution.reshape(shape4), (product, near_r, near_d))
    return tuple(v.reshape(direction.shape) for v in out)


def solution(mesh):
    n_core = 2 if mesh.shape["tm"] % 2 == 0 else 1
    n_x = mesh.shape["tm"] // n_core
    nb = mesh.shape["blk"]
    inner = Mesh(mesh.devices.reshape(nb, n_x, n_core), ("blk", "x", "core"))
    tm = ("x", "core")

    def body(*args):
        direction, legendre = args[2], args[4]
        cycles, time_dev, longitude = direction.shape
        fits = (
            n_core == 2
            and 2 * cycles == LANES
            and time_dev == 2 * PACK
            and nb % 2 == 0
            and longitude % 512 == 0
            and legendre.shape[0] % (4 * CHUNKS) == 0
            and legendre.shape[1] % PACK == 0
            and legendre.shape[2] % LANES == 0
            and args[5].shape[-1] % LANES == 0
        )
        if fits:
            return fast_body(inner, *args)
        return plain_body(*args)

    grid = P("blk", tm, None)
    return jax.shard_map(
        body,
        mesh=inner,
        in_specs=(grid, grid, grid, grid, grid, P(tm, None, None), P()),
        out_specs=(grid, grid, grid),
        check_vma=False,
    )
```

profile of v0, /device:TPU:0, one launch (start us, length us, event | category | flops | bytes accessed | tf_op | source)
XLA Modules:
  0.0 386.0 jit_solution(1795416423640495256)
XLA Ops:
  7.4 14.2 %analysis.2 = (bf16[256,16,128]{2,1,0:T(8,128)(2,1)}, bf16[256,16,128]{2,1,0:T(8,128)(2,1)}, bf16[256,16,128]{2,1,0:T(8,128)(2,1)}) custom-call(f32[64,2,16,1024]{3,2,1,0:T(8,128)} %bitcast.123, f32[64,2,16,1024]{3,2,1,0:T(8,128)} %bitcast.124, f32[64,2,16,1024]{3,2,1,0:T(8,128)} %bitcast.125, f32[64,2,16,1024]{3,2,1,0:T(8,128)} %bitcast.126, ...), custom_call_target="tpu_custom_call" | custom-call | flops 3221225472 | bytes 9961472 | tf_op jit(solution)/shard_map/analysis/pallas_call | solution.py:113
  21.6 33.1 %all_to_all.40.refs_0_ = bf16[8,2,16,16,128]{4,3,2,1,0:T(8,128)(2,1)S(1)} all-to-all(bf16[8,2,16,16,128]{4,3,2,1,0:T(8,128)(2,1)} %bitcast.149), channel_id=1, replica_groups=mesh['blk'=8,'x'=2,'core'=2] {'blk'}, dimensions={0} | all-to-all | bytes 2097152 | tf_op jit(solution)/shard_map/all_to_all | solution.py:514
  59.8 22.8 %collective-permute-done.15.refs_1_ = bf16[8,2,16,16,128]{4,3,2,1,0:T(8,128)(2,1)} collective-permute-done((bf16[8,2,16,16,128]{4,3,2,1,0:T(8,128)(2,1)S(1)}, bf16[8,2,16,16,128]{4,3,2,1,0:T(8,128)(2,1)}, u32[]{:S(2)}, u32[]{:S(2)}) %collective-permute-start.15) | collective-permute-done | bytes 1048608 | tf_op jit(solution)/shard_map/ppermute | solution.py:511
  82.6 9.7 %analysis.3 = bf16[256,16,128]{2,1,0:T(8,128)(2,1)} custom-call(f32[64,2,16,1024]{3,2,1,0:T(8,128)} %bitcast.131, f32[64,2,16,1024]{3,2,1,0:T(8,128)} %bitcast.132, f32[64,2,16,1024]{3,2,1,0:T(8,128)} %bitcast.133, f32[64,2,16,1024]{3,2,1,0:T(8,128)} %bitcast.134, f32[64,2,16,1024]{3,2,1,0:T(8,128)} %bitcast.135, f32[64,2,16,1024]{3,2,1,0:T(8,128)} %bitcast.136, ...), custom_call_target="tpu_custom_call" | custom-call | flops 1073741824 | bytes 8912896 | tf_op jit(solution)/shard_map/analysis/pallas_call | solution.py:113
  92.3 5.7 %all-to-all-start.2 = ((bf16[8,2,16,16,128]{4,3,2,1,0:T(8,128)(2,1)}), bf16[8,2,16,16,128]{4,3,2,1,0:T(8,128)(2,1)S(1)}, u32[]{:S(2)}, u32[]{:S(2)}) async-start(bf16[8,2,16,16,128]{4,3,2,1,0:T(8,128)(2,1)} %bitcast.144), calls=%async_computation.2 | async-start | bytes 2097152 | tf_op jit(solution)/shard_map/all_to_all | solution.py:514
  100.3 6.4 %convert_element_type.187.tmp_ref = bf16[128,128,128]{2,1,0:T(8,128)(2,1)} convert(f32[128,128,128]{2,1,0:T(8,128)} %param.12) | non-fusion elementwise | flops 2097152 | bytes 12582912 | tf_op jit(solution)/shard_map/convert_element_type | solution.py:521
  107.4 16.5 %degrees.7 = (bf16[2,8,2,16,16,128]{5,4,3,2,1,0:T(8,128)(2,1)}, bf16[2,8,2,16,16,128]{5,4,3,2,1,0:T(8,128)(2,1)}) custom-call(s32[25]{0:T(128)} %concatenate.19.sc_ref, bf16[64,128,512]{2,1,0:T(8,128)(2,1)} %leg_ref.7, bf16[128,128,128]{2,1,0:T(8,128)(2,1)} %convert_element_type.187.tmp_ref, bf16[8,2,16,16,128]{4,3,2,1,0:T(8,128)(2,1)} %copy-done.3, ...), custom_call_target="tpu_custom_call" | custom-call | flops 1207959552 | bytes 16777216 | tf_op jit(solution)/shard_map/degrees/pallas_call | solution.py:231
  124.5 5.9 %all-to-all-start = ((bf16[8,2,16,16,128]{4,3,2,1,0:T(8,128)(2,1)}), bf16[8,2,16,16,128]{4,3,2,1,0:T(8,128)(2,1)S(1)}, u32[]{:S(2)}, u32[]{:S(2)}) async-start(bf16[8,2,16,16,128]{4,3,2,1,0:T(8,128)(2,1)} %bitcast.148), calls=%async_computation | async-start | bytes 2097152 | tf_op jit(solution)/shard_map/all_to_all | solution.py:514
  131.7 16.4 %degrees.6 = (bf16[2,8,2,16,16,128]{5,4,3,2,1,0:T(8,128)(2,1)}, bf16[2,8,2,16,16,128]{5,4,3,2,1,0:T(8,128)(2,1)}) custom-call(s32[25]{0:T(128)} %concatenate.18.sc_ref, bf16[64,128,512]{2,1,0:T(8,128)(2,1)} %leg_ref.7, bf16[128,128,128]{2,1,0:T(8,128)(2,1)} %convert_element_type.187.tmp_ref, bf16[8,2,16,16,128]{4,3,2,1,0:T(8,128)(2,1)} %copy-done.2, ...), custom_call_target="tpu_custom_call" | custom-call | flops 1207959552 | bytes 16777216 | tf_op jit(solution)/shard_map/degrees/pallas_call | solution.py:231
  148.6 7.1 %collective-permute-done.5.refs_1_ = bf16[8,2,16,16,128]{4,3,2,1,0:T(8,128)(2,1)} collective-permute-done((bf16[8,2,16,16,128]{4,3,2,1,0:T(8,128)(2,1)S(1)}, bf16[8,2,16,16,128]{4,3,2,1,0:T(8,128)(2,1)}, u32[]{:S(2)}, u32[]{:S(2)}) %collective-permute-start.5) | collective-permute-done | bytes 1048608 | tf_op jit(solution)/shard_map/ppermute | solution.py:511
  162.3 16.6 %degrees.5 = (bf16[2,8,2,16,16,128]{5,4,3,2,1,0:T(8,128)(2,1)}, bf16[2,8,2,16,16,128]{5,4,3,2,1,0:T(8,128)(2,1)}) custom-call(s32[25]{0:T(128)} %concatenate.17.sc_ref, bf16[64,128,512]{2,1,0:T(8,128)(2,1)} %leg_ref.7, bf16[128,128,128]{2,1,0:T(8,128)(2,1)} %convert_element_type.187.tmp_ref, bf16[8,2,16,16,128]{4,3,2,1,0:T(8,128)(2,1)} %copy-done.1, ...), custom_call_target="tpu_custom_call" | custom-call | flops 1207959552 | bytes 16777216 | tf_op jit(solution)/shard_map/degrees/pallas_call | solution.py:231
  178.9 6.1 %collective-permute-done.19 = bf16[8,2,16,16,128]{4,3,2,1,0:T(8,128)(2,1)} collective-permute-done((bf16[8,2,16,16,128]{4,3,2,1,0:T(8,128)(2,1)}, bf16[8,2,16,16,128]{4,3,2,1,0:T(8,128)(2,1)}, u32[]{:S(2)}, u32[]{:S(2)}) %collective-permute-start.19) | collective-permute-done | bytes 1048608 | tf_op jit(solution)/shard_map/ppermute | solution.py:511
  188.2 5.7 %all-to-all-start.7 = ((bf16[8,2,16,16,128]{4,3,2,1,0:T(8,128)(2,1)}), bf16[8,2,16,16,128]{4,3,2,1,0:T(8,128)(2,1)S(1)}, u32[]{:S(2)}, u32[]{:S(2)}) async-start(bf16[8,2,16,16,128]{4,3,2,1,0:T(8,128)(2,1)} %fusion), calls=%async_computation.7 | async-start | bytes 2097152 | tf_op jit(solution)/shard_map/all_to_all | solution.py:514
  194.0 12.9 %collective-permute-done.refs_1_ = bf16[8,2,16,16,128]{4,3,2,1,0:T(8,128)(2,1)} collective-permute-done((bf16[8,2,16,16,128]{4,3,2,1,0:T(8,128)(2,1)S(1)}, bf16[8,2,16,16,128]{4,3,2,1,0:T(8,128)(2,1)}, u32[]{:S(2)}, u32[]{:S(2)}) %collective-permute-start) | collective-permute-done | bytes 1048608 | tf_op jit(solution)/shard_map/ppermute | solution.py:511
  211.0 16.6 %degrees.4 = (bf16[2,8,2,16,16,128]{5,4,3,2,1,0:T(8,128)(2,1)}, bf16[2,8,2,16,16,128]{5,4,3,2,1,0:T(8,128)(2,1)}) custom-call(s32[25]{0:T(128)} %concatenate.16.sc_ref, bf16[64,128,512]{2,1,0:T(8,128)(2,1)} %leg_ref.7, bf16[128,128,128]{2,1,0:T(8,128)(2,1)} %convert_element_type.187.tmp_ref, bf16[8,2,16,16,128]{4,3,2,1,0:T(8,128)(2,1)} %copy-done.4, ...), custom_call_target="tpu_custom_call" | custom-call | flops 1207959552 | bytes 16777216 | tf_op jit(solution)/shard_map/degrees/pallas_call | solution.py:231
  227.7 7.9 %collective-permute-done.14 = bf16[8,2,16,16,128]{4,3,2,1,0:T(8,128)(2,1)} collective-permute-done((bf16[8,2,16,16,128]{4,3,2,1,0:T(8,128)(2,1)}, bf16[8,2,16,16,128]{4,3,2,1,0:T(8,128)(2,1)}, u32[]{:S(2)}, u32[]{:S(2)}) %collective-permute-start.14) | collective-permute-done | bytes 1048608 | tf_op jit(solution)/shard_map/ppermute | solution.py:511
  238.7 5.7 %all-to-all-start.5 = ((bf16[8,2,16,16,128]{4,3,2,1,0:T(8,128)(2,1)}), bf16[8,2,16,16,128]{4,3,2,1,0:T(8,128)(2,1)S(1)}, u32[]{:S(2)}, u32[]{:S(2)}) async-start(bf16[8,2,16,16,128]{4,3,2,1,0:T(8,128)(2,1)} %fusion.1), calls=%async_computation.5 | async-start | bytes 2097152 | tf_op jit(solution)/shard_map/all_to_all | solution.py:514
  247.0 23.9 %collective-permute-done.9 = bf16[8,2,16,16,128]{4,3,2,1,0:T(8,128)(2,1)S(1)} collective-permute-done((bf16[8,2,16,16,128]{4,3,2,1,0:T(8,128)(2,1)S(1)}, bf16[8,2,16,16,128]{4,3,2,1,0:T(8,128)(2,1)S(1)}, u32[]{:S(2)}, u32[]{:S(2)}) %collective-permute-start.9) | collective-permute-done | bytes 1048608 | tf_op jit(solution)/shard_map/ppermute | solution.py:511
  273.6 5.7 %all-to-all-start.3 = ((bf16[8,2,16,16,128]{4,3,2,1,0:T(8,128)(2,1)}), bf16[8,2,16,16,128]{4,3,2,1,0:T(8,128)(2,1)S(1)}, u32[]{:S(2)}, u32[]{:S(2)}) async-start(bf16[8,2,16,16,128]{4,3,2,1,0:T(8,128)(2,1)} %fusion.2), calls=%async_computation.3 | async-start | bytes 2097152 | tf_op jit(solution)/shard_map/all_to_all | solution.py:514
  281.9 22.5 %collective-permute-done.4 = bf16[8,2,16,16,128]{4,3,2,1,0:T(8,128)(2,1)S(1)} collective-permute-done((bf16[8,2,16,16,128]{4,3,2,1,0:T(8,128)(2,1)S(1)}, bf16[8,2,16,16,128]{4,3,2,1,0:T(8,128)(2,1)S(1)}, u32[]{:S(2)}, u32[]{:S(2)}) %collective-permute-start.4) | collective-permute-done | bytes 1048608 | tf_op jit(solution)/shard_map/ppermute | solution.py:511
  307.1 5.7 %all-to-all-start.1 = ((bf16[8,2,16,16,128]{4,3,2,1,0:T(8,128)(2,1)}), bf16[8,2,16,16,128]{4,3,2,1,0:T(8,128)(2,1)S(1)}, u32[]{:S(2)}, u32[]{:S(2)}) async-start(bf16[8,2,16,16,128]{4,3,2,1,0:T(8,128)(2,1)} %fusion.3), calls=%async_computation.1 | async-start | bytes 2097152 | tf_op jit(solution)/shard_map/all_to_all | solution.py:514
  312.8 25.0 %synthesis.2.refs_2_ = f32[64,2,16,1024]{3,2,1,0:T(8,128)} custom-call(bf16[256,16,128]{2,1,0:T(8,128)(2,1)} %bitcast.147, bf16[256,16,128]{2,1,0:T(8,128)(2,1)} %bitcast.146, bf16[256,16,128]{2,1,0:T(8,128)(2,1)} %bitcast.145, bf16[256,1024]{1,0:T(8,128)(2,1)} %get-tuple-element.43.refs_8_.refs_3_, bf16[256,1024]{1,0:T(8,128)(2,1)} %get-tuple-element.46.refs_8_.refs_4_, ...), custom_call_target="tpu_custom_call" | custom-call | flops 3221225472 | bytes 25165824 | tf_op jit(solution)/shard_map/synthesis/pallas_call | solution.py:369
  337.9 19.2 %synthesis.3 = (f32[2,2,4,1024,128]{4,3,2,1,0:T(8,128)S(1)}, f32[8,128]{1,0:T(8,128)S(1)}, f32[2,2,4,1024,128]{4,3,2,1,0:T(8,128)S(1)}, f32[2,2,4,1024,128]{4,3,2,1,0:T(8,128)S(1)}) custom-call(bf16[256,16,128]{2,1,0:T(8,128)(2,1)S(1)} %bitcast.122, bf16[256,1024]{1,0:T(8,128)(2,1)S(1)} %copy-done, f32[64,2,16,1024]{3,2,1,0:T(8,128)} %synthesis.2.refs_2_, ...), custom_call_target="tpu_custom_call" | custom-call | flops 1073741824 | bytes 33554432 | tf_op jit(solution)/shard_map/synthesis/pallas_call | solution.py:369
  373.7 12.3 %update.1 = (f32[64,2,16,1024]{3,2,1,0:T(8,128)}, f32[64,2,16,1024]{3,2,1,0:T(8,128)}, f32[64,2,16,1024]{3,2,1,0:T(8,128)}) custom-call(f32[8,128]{1,0:T(8,128)S(1)} %add.639.refs_0_, f32[8,128]{1,0:T(8,128)S(1)} %collective-permute-done.24.refs_1_, f32[8,128]{1,0:T(8,128)S(1)} %collective-permute-done.25.refs_2_, ...), custom_call_target="tpu_custom_call" | custom-call | flops 12582912 | bytes 33554432 | tf_op jit(solution)/shard_map/update/pallas_call | solution.py:428
  (103 shorter events, 61.5 us)
Async XLA Ops:
  54.7 37.6 %all-to-all-start.4 = ((bf16[8,2,16,16,128]{4,3,2,1,0:T(8,128)(2,1)}), bf16[8,2,16,16,128]{4,3,2,1,0:T(8,128)(2,1)S(1)}, u32[]{:S(2)}, u32[]{:S(2)}) async-start(bf16[8,2,16,16,128]{4,3,2,1,0:T(8,128)(2,1)} %bitcast.20), calls=%async_computation.4 | async-start | bytes 2097152 | tf_op jit(solution)/shard_map/all_to_all | solution.py:514
  58.3 24.4 %collective-permute-start.15 = (bf16[8,2,16,16,128]{4,3,2,1,0:T(8,128)(2,1)S(1)}, bf16[8,2,16,16,128]{4,3,2,1,0:T(8,128)(2,1)}, u32[]{:S(2)}, u32[]{:S(2)}) collective-permute-start(bf16[8,2,16,16,128]{4,3,2,1,0:T(8,128)(2,1)S(1)} %all_to_all.40.refs_0_), channel_id=1, source_target_pairs={{0,2},{2,0},{1,3},{3,1},{4,6},{6,4},{5,7},{7,5},{8,10},{10,8},{9,1... | collective-permute-start | bytes 3145736 | tf_op jit(solution)/shard_map/ppermute | solution.py:511
  59.8 47.6 %collective-permute-start.16 = (bf16[8,2,16,16,128]{4,3,2,1,0:T(8,128)(2,1)S(1)}, bf16[8,2,16,16,128]{4,3,2,1,0:T(8,128)(2,1)}, u32[]{:S(2)}, u32[]{:S(2)}) collective-permute-start(bf16[8,2,16,16,128]{4,3,2,1,0:T(8,128)(2,1)S(1)} %all_to_all.40.refs_0_), channel_id=1, source_target_pairs={{0,1},{1,0},{2,3},{3,2},{4,5},{5,4},{6,7},{7,6},{8,9},{9,8},{10,11... | collective-permute-start | bytes 3145736 | tf_op jit(solution)/shard_map/ppermute | solution.py:526
  82.6 24.7 %collective-permute-start.17 = (bf16[8,2,16,16,128]{4,3,2,1,0:T(8,128)(2,1)}, bf16[8,2,16,16,128]{4,3,2,1,0:T(8,128)(2,1)}, u32[]{:S(2)}, u32[]{:S(2)}) collective-permute-start(bf16[8,2,16,16,128]{4,3,2,1,0:T(8,128)(2,1)} %collective-permute-done.15.refs_1_), channel_id=1, source_target_pairs={{0,1},{1,0},{2,3},{3,2},{4,5},{5,4},{6,7},{7,6},{8,9},{9,8},{10,11... | collective-permute-start | bytes 3145736 | tf_op jit(solution)/shard_map/ppermute | solution.py:526
  92.3 32.2 %all-to-all-start.2 = ((bf16[8,2,16,16,128]{4,3,2,1,0:T(8,128)(2,1)}), bf16[8,2,16,16,128]{4,3,2,1,0:T(8,128)(2,1)S(1)}, u32[]{:S(2)}, u32[]{:S(2)}) async-start(bf16[8,2,16,16,128]{4,3,2,1,0:T(8,128)(2,1)} %bitcast.144), calls=%async_computation.2 | async-start | bytes 2097152 | tf_op jit(solution)/shard_map/all_to_all | solution.py:514
  98.1 26.3 %collective-permute-start.10 = (bf16[8,2,16,16,128]{4,3,2,1,0:T(8,128)(2,1)S(1)}, bf16[8,2,16,16,128]{4,3,2,1,0:T(8,128)(2,1)}, u32[]{:S(2)}, u32[]{:S(2)}) collective-permute-start(bf16[8,2,16,16,128]{4,3,2,1,0:T(8,128)(2,1)S(1)} %all-to-all-done.4.refs_0_), channel_id=1, source_target_pairs={{0,2},{2,0},{1,3},{3,1},{4,6},{6,4},{5,7},{7,5},{8,10},{10,8},{9,1... | collective-permute-start | bytes 3145736 | tf_op jit(solution)/shard_map/ppermute | solution.py:511
  123.8 31.9 %collective-permute-start.18 = (bf16[2,8,2,16,16,128]{5,4,3,2,1,0:T(8,128)(2,1)}, bf16[2,8,2,16,16,128]{5,4,3,2,1,0:T(8,128)(2,1)}, u32[]{:S(2)}, u32[]{:S(2)}) collective-permute-start(bf16[2,8,2,16,16,128]{5,4,3,2,1,0:T(8,128)(2,1)} %get-tuple-element.31), channel_id=1, source_target_pairs={{0,1},{1,0},{2,3},{3,2},{4,5},{5,4},{6,7},{7,6},{8,9},{9,8},{10,11... | collective-permute-start | bytes 6291464 | tf_op jit(solution)/shard_map/ppermute | solution.py:529
  123.9 7.8 %collective-permute-start.11 = (bf16[8,2,16,16,128]{4,3,2,1,0:T(8,128)(2,1)S(1)}, bf16[8,2,16,16,128]{4,3,2,1,0:T(8,128)(2,1)}, u32[]{:S(2)}, u32[]{:S(2)}) collective-permute-start(bf16[8,2,16,16,128]{4,3,2,1,0:T(8,128)(2,1)S(1)} %all-to-all-done.4.refs_0_), channel_id=1, source_target_pairs={{0,1},{1,0},{2,3},{3,2},{4,5},{5,4},{6,7},{7,6},{8,9},{9,8},{10,11... | collective-permute-start | bytes 3145736 | tf_op jit(solution)/shard_map/ppermute | solution.py:526
  124.5 34.6 %all-to-all-start = ((bf16[8,2,16,16,128]{4,3,2,1,0:T(8,128)(2,1)}), bf16[8,2,16,16,128]{4,3,2,1,0:T(8,128)(2,1)S(1)}, u32[]{:S(2)}, u32[]{:S(2)}) async-start(bf16[8,2,16,16,128]{4,3,2,1,0:T(8,128)(2,1)} %bitcast.148), calls=%async_computation | async-start | bytes 2097152 | tf_op jit(solution)/shard_map/all_to_all | solution.py:514
  130.4 25.3 %collective-permute-start.5 = (bf16[8,2,16,16,128]{4,3,2,1,0:T(8,128)(2,1)S(1)}, bf16[8,2,16,16,128]{4,3,2,1,0:T(8,128)(2,1)}, u32[]{:S(2)}, u32[]{:S(2)}) collective-permute-start(bf16[8,2,16,16,128]{4,3,2,1,0:T(8,128)(2,1)S(1)} %all-to-all-done.2.refs_0_), channel_id=1, source_target_pairs={{0,2},{2,0},{1,3},{3,1},{4,6},{6,4},{5,7},{7,5},{8,10},{10,8},{9,1... | collective-permute-start | bytes 3145736 | tf_op jit(solution)/shard_map/ppermute | solution.py:511
  148.1 58.8 %collective-permute-start.13 = (bf16[2,8,2,16,16,128]{5,4,3,2,1,0:T(8,128)(2,1)}, bf16[2,8,2,16,16,128]{5,4,3,2,1,0:T(8,128)(2,1)}, u32[]{:S(2)}, u32[]{:S(2)}) collective-permute-start(bf16[2,8,2,16,16,128]{5,4,3,2,1,0:T(8,128)(2,1)} %get-tuple-element.28), channel_id=1, source_target_pairs={{0,1},{1,0},{2,3},{3,2},{4,5},{5,4},{6,7},{7,6},{8,9},{9,8},{10,11... | collective-permute-start | bytes 6291464 | tf_op jit(solution)/shard_map/ppermute | solution.py:529
  148.1 13.2 %collective-permute-start.6 = (bf16[8,2,16,16,128]{4,3,2,1,0:T(8,128)(2,1)S(1)}, bf16[8,2,16,16,128]{4,3,2,1,0:T(8,128)(2,1)S(1)}, u32[]{:S(2)}, u32[]{:S(2)}) collective-permute-start(bf16[8,2,16,16,128]{4,3,2,1,0:T(8,128)(2,1)S(1)} %all-to-all-done.2.refs_0_), channel_id=1, source_target_pairs={{0,1},{1,0},{2,3},{3,2},{4,5},{5,4},{6,7},{7,6},{8,9},{9,8},{10,11... | collective-permute-start | bytes 3145736 | tf_op jit(solution)/shard_map/ppermute | solution.py:526
  158.6 26.3 %collective-permute-start.19 = (bf16[8,2,16,16,128]{4,3,2,1,0:T(8,128)(2,1)}, bf16[8,2,16,16,128]{4,3,2,1,0:T(8,128)(2,1)}, u32[]{:S(2)}, u32[]{:S(2)}) collective-permute-start(bf16[8,2,16,16,128]{4,3,2,1,0:T(8,128)(2,1)} %fusion.35), channel_id=1, source_target_pairs={{0,2},{2,0},{1,3},{3,1},{4,6},{6,4},{5,7},{7,5},{8,10},{10,8},{9,1... | collective-permute-start | bytes 3145736 | tf_op jit(solution)/shard_map/ppermute | solution.py:511
  159.1 47.8 %collective-permute-start = (bf16[8,2,16,16,128]{4,3,2,1,0:T(8,128)(2,1)S(1)}, bf16[8,2,16,16,128]{4,3,2,1,0:T(8,128)(2,1)}, u32[]{:S(2)}, u32[]{:S(2)}) collective-permute-start(bf16[8,2,16,16,128]{4,3,2,1,0:T(8,128)(2,1)S(1)} %all-to-all-done.refs_0_), channel_id=1, source_target_pairs={{0,2},{2,0},{1,3},{3,1},{4,6},{6,4},{5,7},{7,5},{8,10},{10,8},{9,1... | collective-permute-start | bytes 3145736 | tf_op jit(solution)/shard_map/ppermute | solution.py:511
  178.8 65.6 %collective-permute-start.8 = (bf16[2,8,2,16,16,128]{5,4,3,2,1,0:T(8,128)(2,1)}, bf16[2,8,2,16,16,128]{5,4,3,2,1,0:T(8,128)(2,1)}, u32[]{:S(2)}, u32[]{:S(2)}) collective-permute-start(bf16[2,8,2,16,16,128]{5,4,3,2,1,0:T(8,128)(2,1)} %get-tuple-element.25), channel_id=1, source_target_pairs={{0,1},{1,0},{2,3},{3,2},{4,5},{5,4},{6,7},{7,6},{8,9},{9,8},{10,11... | collective-permute-start | bytes 6291464 | tf_op jit(solution)/shard_map/ppermute | solution.py:529
  188.2 50.5 %all-to-all-start.7 = ((bf16[8,2,16,16,128]{4,3,2,1,0:T(8,128)(2,1)}), bf16[8,2,16,16,128]{4,3,2,1,0:T(8,128)(2,1)S(1)}, u32[]{:S(2)}, u32[]{:S(2)}) async-start(bf16[8,2,16,16,128]{4,3,2,1,0:T(8,128)(2,1)} %fusion), calls=%async_computation.7 | async-start | bytes 2097152 | tf_op jit(solution)/shard_map/all_to_all | solution.py:514
  193.9 17.0 %collective-permute-start.1 = (bf16[8,2,16,16,128]{4,3,2,1,0:T(8,128)(2,1)S(1)}, bf16[8,2,16,16,128]{4,3,2,1,0:T(8,128)(2,1)}, u32[]{:S(2)}, u32[]{:S(2)}) collective-permute-start(bf16[8,2,16,16,128]{4,3,2,1,0:T(8,128)(2,1)S(1)} %all-to-all-done.refs_0_), channel_id=1, source_target_pairs={{0,1},{1,0},{2,3},{3,2},{4,5},{5,4},{6,7},{7,6},{8,9},{9,8},{10,11... | collective-permute-start | bytes 3145736 | tf_op jit(solution)/shard_map/ppermute | solution.py:526
  209.8 25.9 %collective-permute-start.14 = (bf16[8,2,16,16,128]{4,3,2,1,0:T(8,128)(2,1)}, bf16[8,2,16,16,128]{4,3,2,1,0:T(8,128)(2,1)}, u32[]{:S(2)}, u32[]{:S(2)}) collective-permute-start(bf16[8,2,16,16,128]{4,3,2,1,0:T(8,128)(2,1)} %fusion.33), channel_id=1, source_target_pairs={{0,2},{2,0},{1,3},{3,1},{4,6},{6,4},{5,7},{7,5},{8,10},{10,8},{9,1... | collective-permute-start | bytes 3145736 | tf_op jit(solution)/shard_map/ppermute | solution.py:511
  227.5 51.8 %collective-permute-start.3 = (bf16[2,8,2,16,16,128]{5,4,3,2,1,0:T(8,128)(2,1)}, bf16[2,8,2,16,16,128]{5,4,3,2,1,0:T(8,128)(2,1)}, u32[]{:S(2)}, u32[]{:S(2)}) collective-permute-start(bf16[2,8,2,16,16,128]{5,4,3,2,1,0:T(8,128)(2,1)} %get-tuple-element.23), channel_id=1, source_target_pairs={{0,1},{1,0},{2,3},{3,2},{4,5},{5,4},{6,7},{7,6},{8,9},{9,8},{10,11... | collective-permute-start | bytes 6291464 | tf_op jit(solution)/shard_map/ppermute | solution.py:529
  238.7 34.9 %all-to-all-start.5 = ((bf16[8,2,16,16,128]{4,3,2,1,0:T(8,128)(2,1)}), bf16[8,2,16,16,128]{4,3,2,1,0:T(8,128)(2,1)S(1)}, u32[]{:S(2)}, u32[]{:S(2)}) async-start(bf16[8,2,16,16,128]{4,3,2,1,0:T(8,128)(2,1)} %fusion.1), calls=%async_computation.5 | async-start | bytes 2097152 | tf_op jit(solution)/shard_map/all_to_all | solution.py:514
  246.4 24.5 %collective-permute-start.9 = (bf16[8,2,16,16,128]{4,3,2,1,0:T(8,128)(2,1)S(1)}, bf16[8,2,16,16,128]{4,3,2,1,0:T(8,128)(2,1)S(1)}, u32[]{:S(2)}, u32[]{:S(2)}) collective-permute-start(bf16[8,2,16,16,128]{4,3,2,1,0:T(8,128)(2,1)S(1)} %fusion.31), channel_id=1, source_target_pairs={{0,2},{2,0},{1,3},{3,1},{4,6},{6,4},{5,7},{7,5},{8,10},{10,8},{9,1... | collective-permute-start | bytes 3145736 | tf_op jit(solution)/shard_map/ppermute | solution.py:511
  273.6 33.5 %all-to-all-start.3 = ((bf16[8,2,16,16,128]{4,3,2,1,0:T(8,128)(2,1)}), bf16[8,2,16,16,128]{4,3,2,1,0:T(8,128)(2,1)S(1)}, u32[]{:S(2)}, u32[]{:S(2)}) async-start(bf16[8,2,16,16,128]{4,3,2,1,0:T(8,128)(2,1)} %fusion.2), calls=%async_computation.3 | async-start | bytes 2097152 | tf_op jit(solution)/shard_map/all_to_all | solution.py:514
  281.3 23.1 %collective-permute-start.4 = (bf16[8,2,16,16,128]{4,3,2,1,0:T(8,128)(2,1)S(1)}, bf16[8,2,16,16,128]{4,3,2,1,0:T(8,128)(2,1)S(1)}, u32[]{:S(2)}, u32[]{:S(2)}) collective-permute-start(bf16[8,2,16,16,128]{4,3,2,1,0:T(8,128)(2,1)S(1)} %fusion.29), channel_id=1, source_target_pairs={{0,2},{2,0},{1,3},{3,1},{4,6},{6,4},{5,7},{7,5},{8,10},{10,8},{9,1... | collective-permute-start | bytes 3145736 | tf_op jit(solution)/shard_map/ppermute | solution.py:511
  307.1 30.8 %all-to-all-start.1 = ((bf16[8,2,16,16,128]{4,3,2,1,0:T(8,128)(2,1)}), bf16[8,2,16,16,128]{4,3,2,1,0:T(8,128)(2,1)S(1)}, u32[]{:S(2)}, u32[]{:S(2)}) async-start(bf16[8,2,16,16,128]{4,3,2,1,0:T(8,128)(2,1)} %fusion.3), calls=%async_computation.1 | async-start | bytes 2097152 | tf_op jit(solution)/shard_map/all_to_all | solution.py:514
  (22 other events, 295.0 us)
where the time goes:
time: 388 us; the launch traced here: 386 us
  Pallas kernels  146 us (38%)
  waiting for transfers between devices  112 us (29%)
  starting transfers between devices  54.7 us (14%)
  other arithmetic  33.4 us (9%)
  blocking collectives  33.1 us (9%)
  local copies, waits for them, and re-layouts  5.41 us (1%)
    ppermute x8, waiting for transfers between devices, shift(): return lax.ppermute(v, 'x', [(i, (i + s) % n_x) for i in range(n_x)])  103 us
    pallas_call x4, Pallas kernels, degree_call(): pl.pallas_call(kernel, out_shape=(out_shape, out_shape), grid_spec=pltpu....  66 us
    pallas_call x2, Pallas kernels, synthesis_call(): pl.pallas_call(kernel, out_shape=tuple(out_shape), grid=(hi_n // sub, len...  44.3 us
    all_to_all x7, starting transfers between devices, across(): return lax.all_to_all(v, 'blk', split_axis=0, concat_axis=0, tiled=True)  38.1 us
    all_to_all x1, blocking collectives, across(): return lax.all_to_all(v, 'blk', split_axis=0, concat_axis=0, tiled=True)  33.1 us
    pallas_call x2, Pallas kernels, analysis_call(): pl.pallas_call(kernel, out_shape=(out,) * n_tab, grid=(steps,), in_specs=...  23.9 us
    pallas_call x1, Pallas kernels, update_call(): pl.pallas_call(kernel, out_shape=(jax.ShapeDtypeStruct(solution4.shape, F...  12.3 us
    convert_element_type x4, other arithmetic, fast_body(): total = total.astype(BF)  11.6 us
  transfers between devices with their start and end apart: 34, of which 14 were waited for; matrix products, arithmetic and copies ran while one was open for 8% of the time, Pallas kernels for 26%

commit v1 on v0

--- a/solution.py
+++ b/solution.py
@@ -10,7 +10,8 @@
 
 LANES = 128
 PACK = 16
-CHUNKS = 4
+PLAN = ((0, 0), (1, 0), (1, 1), (0, 1))
+CHUNKS = len(PLAN)
 BF = jnp.bfloat16
 F32 = jnp.float32
 
@@ -131,30 +132,32 @@
     )(*[direction4] * parts_n, *tables)
 
 
-def degree_call(scalars, legendre, temporal, gathered, chunk, n_x):
+def degree_call(scalars, legendre, temporal, gathered, n_x):
     _, deg_dev, lat_all = legendre.shape
     time_all = temporal.shape[-1]
     n_pieces = len(gathered)
     nb, _, chunk_n, hi_n, _ = gathered[0].shape
     time_dev = 2 * hi_n
-    kb = 4
-    lb = 16
+    kb = 8
+    lb = 32
     n1 = chunk_n // kb
     n2 = deg_dev // lb
     pitch = deg_dev + 8
     rows = 2 * time_all
-    first = chunk * n1
-
-    def kernel(sc_ref, leg_ref, tmp_ref, *refs):
+    order_at = 1 + 2 * n_pieces
+    row_at = order_at + chunk_n
+
+    def kernel(sc_ref, *refs):
+        leg_refs, tmp_ref, refs = refs[:kb], refs[kb], refs[kb + 1 :]
         r_refs = refs[:n_pieces]
         keep_ref, send_ref, c_ref, r_scr, g_scr = refs[n_pieces:]
         step = pl.program_id(0)
         low = low_half((hi_n, LANES))
 
         def masked(kk, k):
-            order = sc_ref[1 + 2 * n_pieces + k]
+            order = sc_ref[order_at + k]
             degree = sc_ref[0] + lax.broadcasted_iota(jnp.int32, (deg_dev, lat_all), 0)
-            values = leg_ref[kk]
+            values = leg_refs[kk][0]
             return jnp.where(degree >= order, values, jnp.zeros_like(values))
 
         @pl.when(step < n1)
@@ -214,12 +217,12 @@
                             out[q % n_x, 2 * p, c, kk] = jnp.where(low, v0, swap_halves(v1))
                             out[q % n_x, 2 * p + 1, c, kk] = jnp.where(low, swap_halves(v0), v1)
 
-    def leg_map(s, sc):
-        return (
-            first + jnp.where(s < n1, s, jnp.where(s < n1 + n2, n1 - 1, s - n1 - n2)),
-            0,
-            0,
-        )
+    def leg_spec(kk):
+        def index(s, sc):
+            step = jnp.where(s < n1, s, jnp.where(s < n1 + n2, n1 - 1, s - n1 - n2))
+            return (sc[row_at + step * kb + kk], 0, 0)
+
+        return pl.BlockSpec((1, deg_dev, lat_all), index)
 
     piece = (nb, 2, chunk_n, hi_n, LANES)
     out_block = pl.BlockSpec(
@@ -234,8 +237,8 @@
         grid_spec=pltpu.PrefetchScalarGridSpec(
             num_scalar_prefetch=1,
             grid=(n1 + n2 + n1,),
-            in_specs=[
-                pl.BlockSpec((kb, deg_dev, lat_all), leg_map),
+            in_specs=[leg_spec(kk) for kk in range(kb)]
+            + [
                 pl.BlockSpec(
                     (lb, time_all, time_all),
                     lambda s, sc: (jnp.clip(s - n1, 0, n2 - 1), 0, 0),
@@ -264,7 +267,7 @@
             transcendentals=0,
         ),
         name="degrees",
-    )(scalars, legendre, temporal, *gathered)
+    )(scalars, *[legendre] * kb, temporal, *gathered)
 
 
 def synthesis_call(received, tables, previous, fields, scale):
@@ -275,6 +278,7 @@
     cycles = LANES // lo_n
     sub = 8
     jb = 512
+    batch = 4
     last = previous is not None
     n_grid = 3 if last else 2
 
@@ -301,24 +305,31 @@
             if last:
                 sum_ref[...] = jnp.zeros_like(sum_ref)
 
-        def one(i, carry):
+        def some(i, carry):
             y = None
             for n in range(n_tab):
-                at = pl.ds(n * cols * hi_n + h * sub + i, cols, stride=hi_n)
-                v = s_ref[at, :].astype(BF)
+                parts = []
+                for ii in range(batch):
+                    at = n * cols * hi_n + h * sub + i * batch + ii
+                    parts.append(s_ref[pl.ds(at, cols, stride=hi_n), :].astype(BF))
                 term = lax.dot_general(
-                    v, tab_refs[n][...], (((0,), (0,)), ((), ())), preferred_element_type=F32
+                    jnp.concatenate(parts, axis=1),
+                    tab_refs[n][...],
+                    (((0,), (0,)), ((), ())),
+                    preferred_element_type=F32,
                 )
                 y = term if y is None else y + term
             y = y * scale
-            for lo in range(lo_n):
-                for part in range(jb // LANES):
-                    p_ref[part, pl.ds(lo * sub + i, cycles, stride=lo_n * sub), :] = y[
-                        lo * cycles : (lo + 1) * cycles, part * LANES : (part + 1) * LANES
-                    ]
+            for ii in range(batch):
+                for lo in range(lo_n):
+                    at = pl.ds(lo * sub + i * batch + ii, cycles, stride=lo_n * sub)
+                    rows = slice((ii * lo_n + lo) * cycles, (ii * lo_n + lo + 1) * cycles)
+                    for part in range(jb // LANES):
+                        lanes = slice(part * LANES, (part + 1) * LANES)
+                        p_ref[part, at, :] = y[rows, lanes]
             return carry
 
-        lax.fori_loop(0, sub, one, 0)
+        lax.fori_loop(0, sub // batch, some, 0)
         group = 8
 
         def finish(i, carry):
@@ -488,14 +499,21 @@
     chunk_n = per_device // CHUNKS
     cols = nb * 2 * chunk_n
     blk_i, x_i, core_i = (lax.axis_index(name) for name in ("blk", "x", "core"))
-    grouped = order_table.reshape(nb, per_device)
-    own_orders = lax.dynamic_slice_in_dim(order_table, blk_i * per_device, per_device)
+    half = per_device // 2
+    halves_of = order_table.reshape(nb, 2, half)
+    grouped = jnp.stack([jnp.min(halves_of, axis=1), jnp.max(halves_of, axis=1)])
+    own = lax.dynamic_slice_in_dim(halves_of, blk_i, 1)[0]
+    slots = jnp.arange(half, dtype=jnp.int32)
+    flip = jnp.where(own[0] < own[1], 0, half)
+    own_rows = jnp.stack([slots + flip, slots + half - flip])
+    own_orders = jnp.stack([jnp.min(own, axis=0), jnp.max(own, axis=0)])
     shape4 = (cycles, lo_n, hi_n, longitude)
     direction4, noise4, residual4 = (v.reshape(shape4) for v in (direction, noise_var, residual))
     quarter = (longitude // 4) * 3
 
     def table_of(chunk):
-        orders = grouped[:, chunk * chunk_n : (chunk + 1) * chunk_n]
+        high, start = PLAN[chunk]
+        orders = grouped[high][:, start * chunk_n : (start + 1) * chunk_n]
         points = jnp.arange(longitude, dtype=jnp.int32)
         turn = jnp.arange(2, dtype=jnp.int32) * quarter
         phases = orders[:, None, :, None] * points + turn[None, :, None, None]
@@ -507,8 +525,9 @@
     header = jnp.stack([base] + forth + back).astype(jnp.int32)
     swap = [(i, (i + 1) % n_core) for i in range(n_core)]
 
-    def shift(v, s):
-        return lax.ppermute(v, "x", [(i, (i + s) % n_x) for i in range(n_x)])
+    def shift(v, s, keep):
+        pairs = [(i, (i + s) % n_x) for i in range(n_x)]
+        return lax.ppermute(v, "x", [pair for pair in pairs if keep(*pair)])
 
     def across(v):
         return lax.all_to_all(v, "blk", split_axis=0, concat_axis=0, tiled=True)
@@ -520,16 +539,24 @@
     spectra += list(analysis_call(direction4, tables[1:]))
     temporal_narrow = temporal.astype(BF)
     received = []
-    for g in range(CHUNKS):
+    for g, (high, start) in enumerate(PLAN):
+
+        def forward(source, target):
+            return target > 0 or not high
+
+        def backward(source, target):
+            return source > 0 or not high
+
         mine = across(spectra[g].reshape(piece))
-        own = [mine] + [shift(mine, s) for s in range(1, n_x)]
+        own = [mine] + [shift(mine, s, forward) for s in range(1, n_x)]
         pieces = own + [lax.ppermute(v, "core", swap) for v in own]
-        scalars = jnp.concatenate([header, own_orders[g * chunk_n : (g + 1) * chunk_n]])
-        keep, send = degree_call(scalars, legendre, temporal_narrow, pieces, g, n_x)
+        span = slice(start * chunk_n, (start + 1) * chunk_n)
+        scalars = jnp.concatenate([header, own_orders[high, span], own_rows[high, span]])
+        keep, send = degree_call(scalars, legendre, temporal_narrow, pieces, n_x)
         other = lax.ppermute(send, "core", swap)
         halves = [keep[s].astype(F32) + other[s].astype(F32) for s in range(n_x)]
         halves = [halves[0].astype(BF)] + [v.astype(BF) for v in halves[1:]]
-        parts = [shift(halves[s], s) for s in range(1, n_x)]
+        parts = [shift(halves[s], s, backward) for s in range(1, n_x)]
         total = halves[0].astype(F32)
         for part in parts:
             total = total + part.astype(F32)
@@ -557,11 +584,12 @@
         cycles, time_dev, longitude = direction.shape
         fits = (
             n_core == 2
+            and n_x == 2
             and 2 * cycles == LANES
             and time_dev == 2 * PACK
             and nb % 2 == 0
             and longitude % 512 == 0
-            and legendre.shape[0] % (4 * CHUNKS) == 0
+            and legendre.shape[0] % (8 * CHUNKS) == 0
             and legendre.shape[1] % PACK == 0
             and legendre.shape[2] % LANES == 0
             and args[5].shape[-1] % LANES == 0

time: 388 us -> 384 us (0.990)
  Pallas kernels: 146 us -> 125 us
  waiting for transfers between devices: 112 us -> 123 us
  starting transfers between devices: 54.7 us -> 63.1 us
    ppermute x8, starting transfers between devices: 7.32 us -> 18.8 us  [shift(): return lax.ppermute(v, 'x', [pair for pair in pairs if keep(*pair)])]
    pallas_call x2, Pallas kernels: 44.3 us -> 33.1 us  [synthesis_call(): pl.pallas_call(kernel, out_shape=tuple(out_shape), grid=(hi_n // sub, len...]
    pallas_call x4, Pallas kernels: 66 us -> 55.4 us  [degree_call(): pl.pallas_call(kernel, out_shape=(out_shape, out_shape), grid_spec=pltpu....]
    ppermute x8, waiting for transfers between devices: 103 us -> 109 us  [shift(): return lax.ppermute(v, 'x', [pair for pair in pairs if keep(*pair)])]
    all_to_all x7, waiting for transfers between devices: 0.08 us -> 4.09 us  [across(): return lax.all_to_all(v, 'blk', split_axis=0, concat_axis=0, tiled=True)]
  transfers between devices with their start and end apart: 34 -> 34, of which waited for: 14 -> 16; matrix products, arithmetic and copies ran while one was open for 8% -> 8% of each run, Pallas kernels for 26% -> 22%
where the time goes in v1:
time: 384 us; the launch traced here: 383 us
  Pallas kernels  125 us (33%)
  waiting for transfers between devices  123 us (32%)
  starting transfers between devices  63.1 us (16%)
  other arithmetic  33.5 us (9%)
  blocking collectives  33.1 us (9%)
  local copies, waits for them, and re-layouts  4.79 us (1%)
    ppermute x8, waiting for transfers between devices, shift(): return lax.ppermute(v, 'x', [pair for pair in pairs if keep(*pair)])  109 us
    pallas_call x4, Pallas kernels, degree_call(): pl.pallas_call(kernel, out_shape=(out_shape, out_shape), grid_spec=pltpu....  55.4 us
    all_to_all x7, starting transfers between devices, across(): return lax.all_to_all(v, 'blk', split_axis=0, concat_axis=0, tiled=True)  38.1 us
    pallas_call x2, Pallas kernels, synthesis_call(): pl.pallas_call(kernel, out_shape=tuple(out_shape), grid=(hi_n // sub, len...  33.1 us
    all_to_all x1, blocking collectives, across(): return lax.all_to_all(v, 'blk', split_axis=0, concat_axis=0, tiled=True)  33.1 us
    pallas_call x2, Pallas kernels, analysis_call(): pl.pallas_call(kernel, out_shape=(out,) * n_tab, grid=(steps,), in_specs=...  23.9 us
    ppermute x8, starting transfers between devices, shift(): return lax.ppermute(v, 'x', [pair for pair in pairs if keep(*pair)])  18.8 us
    pallas_call x1, Pallas kernels, update_call(): pl.pallas_call(kernel, out_shape=(jax.ShapeDtypeStruct(solution4.shape, F...  12.3 us
  transfers between devices with their start and end apart: 34, of which 16 were waited for; matrix products, arithmetic and copies ran while one was open for 8% of the time, Pallas kernels for 22%

profile of v1, /device:TPU:0, one launch (start us, length us, event | category | flops | bytes accessed | tf_op | source)
XLA Modules:
  0.0 382.8 jit_solution(4376761158154365167)
XLA Ops:
  7.5 14.2 %analysis.2 = (bf16[256,16,128]{2,1,0:T(8,128)(2,1)}, bf16[256,16,128]{2,1,0:T(8,128)(2,1)}, bf16[256,16,128]{2,1,0:T(8,128)(2,1)}) custom-call(f32[64,2,16,1024]{3,2,1,0:T(8,128)} %bitcast.144, f32[64,2,16,1024]{3,2,1,0:T(8,128)} %bitcast.145, f32[64,2,16,1024]{3,2,1,0:T(8,128)} %bitcast.146, f32[64,2,16,1024]{3,2,1,0:T(8,128)} %bitcast.147, ...), custom_call_target="tpu_custom_call" | custom-call | flops 3221225472 | bytes 9961472 | tf_op jit(solution)/shard_map/analysis/pallas_call | solution.py:114
  21.7 33.1 %all_to_all.40.refs_9_ = bf16[8,2,16,16,128]{4,3,2,1,0:T(8,128)(2,1)S(1)} all-to-all(bf16[8,2,16,16,128]{4,3,2,1,0:T(8,128)(2,1)} %bitcast.170), channel_id=1, replica_groups=mesh['blk'=8,'x'=2,'core'=2] {'blk'}, dimensions={0} | all-to-all | bytes 2097152 | tf_op jit(solution)/shard_map/all_to_all | solution.py:533
  62.8 20.8 %collective-permute-done.15.refs_10_ = bf16[8,2,16,16,128]{4,3,2,1,0:T(8,128)(2,1)} collective-permute-done((bf16[8,2,16,16,128]{4,3,2,1,0:T(8,128)(2,1)S(1)}, bf16[8,2,16,16,128]{4,3,2,1,0:T(8,128)(2,1)}, u32[]{:S(2)}, u32[]{:S(2)}) %collective-permute-start.15) | collective-permute-done | bytes 1048608 | tf_op jit(solution)/shard_map/ppermute | solution.py:530
  83.6 9.7 %analysis.3 = bf16[256,16,128]{2,1,0:T(8,128)(2,1)} custom-call(f32[64,2,16,1024]{3,2,1,0:T(8,128)} %bitcast.152, f32[64,2,16,1024]{3,2,1,0:T(8,128)} %bitcast.153, f32[64,2,16,1024]{3,2,1,0:T(8,128)} %bitcast.154, f32[64,2,16,1024]{3,2,1,0:T(8,128)} %bitcast.155, f32[64,2,16,1024]{3,2,1,0:T(8,128)} %bitcast.156, f32[64,2,16,1024]{3,2,1,0:T(8,128)} %bitcast.157, ...), custom_call_target="tpu_custom_call" | custom-call | flops 1073741824 | bytes 8912896 | tf_op jit(solution)/shard_map/analysis/pallas_call | solution.py:114
  93.2 5.7 %all-to-all-start.2 = ((bf16[8,2,16,16,128]{4,3,2,1,0:T(8,128)(2,1)}), bf16[8,2,16,16,128]{4,3,2,1,0:T(8,128)(2,1)S(1)}, u32[]{:S(2)}, u32[]{:S(2)}) async-start(bf16[8,2,16,16,128]{4,3,2,1,0:T(8,128)(2,1)} %bitcast.165), calls=%async_computation.2 | async-start | bytes 2097152 | tf_op jit(solution)/shard_map/all_to_all | solution.py:533
  104.5 6.4 %convert_element_type.187.refs_8_ = bf16[128,128,128]{2,1,0:T(8,128)(2,1)} convert(f32[128,128,128]{2,1,0:T(8,128)} %param.12) | non-fusion elementwise | flops 2097152 | bytes 12582912 | tf_op jit(solution)/shard_map/convert_element_type | solution.py:540
  111.7 13.9 %degrees.7 = (bf16[2,8,2,16,16,128]{5,4,3,2,1,0:T(8,128)(2,1)}, bf16[2,8,2,16,16,128]{5,4,3,2,1,0:T(8,128)(2,1)}) custom-call(s32[41]{0:T(128)} %concatenate.19.sc_ref, bf16[64,128,512]{2,1,0:T(8,128)(2,1)} %refs_7_.7, bf16[64,128,512]{2,1,0:T(8,128)(2,1)} %refs_7_.7, bf16[64,128,512]{2,1,0:T(8,128)(2,1)} %refs_7_.7, bf16[64,128,512]{2,1,0:T(8,128)(2,1)} %refs_7_.7, ...), custom_call_target="tpu_custom_call" | custom-call | flops 1207959552 | bytes 16777216 | tf_op jit(solution)/shard_map/degrees/pallas_call | solution.py:234
  126.3 5.9 %all-to-all-start = ((bf16[8,2,16,16,128]{4,3,2,1,0:T(8,128)(2,1)}), bf16[8,2,16,16,128]{4,3,2,1,0:T(8,128)(2,1)S(1)}, u32[]{:S(2)}, u32[]{:S(2)}) async-start(bf16[8,2,16,16,128]{4,3,2,1,0:T(8,128)(2,1)} %bitcast.169), calls=%async_computation | async-start | bytes 2097152 | tf_op jit(solution)/shard_map/all_to_all | solution.py:533
  135.2 13.8 %degrees.6 = (bf16[2,8,2,16,16,128]{5,4,3,2,1,0:T(8,128)(2,1)}, bf16[2,8,2,16,16,128]{5,4,3,2,1,0:T(8,128)(2,1)}) custom-call(s32[41]{0:T(128)} %concatenate.18.sc_ref, bf16[64,128,512]{2,1,0:T(8,128)(2,1)} %refs_7_.7, bf16[64,128,512]{2,1,0:T(8,128)(2,1)} %refs_7_.7, bf16[64,128,512]{2,1,0:T(8,128)(2,1)} %refs_7_.7, bf16[64,128,512]{2,1,0:T(8,128)(2,1)} %refs_7_.7, ...), custom_call_target="tpu_custom_call" | custom-call | flops 1207959552 | bytes 16777216 | tf_op jit(solution)/shard_map/degrees/pallas_call | solution.py:234
  149.6 8.6 %collective-permute-done.5.refs_10_ = bf16[8,2,16,16,128]{4,3,2,1,0:T(8,128)(2,1)} collective-permute-done((bf16[8,2,16,16,128]{4,3,2,1,0:T(8,128)(2,1)S(1)}, bf16[8,2,16,16,128]{4,3,2,1,0:T(8,128)(2,1)}, u32[]{:S(2)}, u32[]{:S(2)}) %collective-permute-start.5) | collective-permute-done | bytes 1048608 | tf_op jit(solution)/shard_map/ppermute | solution.py:530
  167.7 13.8 %degrees.5 = (bf16[2,8,2,16,16,128]{5,4,3,2,1,0:T(8,128)(2,1)}, bf16[2,8,2,16,16,128]{5,4,3,2,1,0:T(8,128)(2,1)}) custom-call(s32[41]{0:T(128)} %concatenate.17.sc_ref, bf16[64,128,512]{2,1,0:T(8,128)(2,1)} %refs_7_.7, bf16[64,128,512]{2,1,0:T(8,128)(2,1)} %refs_7_.7, bf16[64,128,512]{2,1,0:T(8,128)(2,1)} %refs_7_.7, bf16[64,128,512]{2,1,0:T(8,128)(2,1)} %refs_7_.7, ...), custom_call_target="tpu_custom_call" | custom-call | flops 1207959552 | bytes 16777216 | tf_op jit(solution)/shard_map/degrees/pallas_call | solution.py:234
  181.6 7.7 %collective-permute-done.19 = bf16[8,2,16,16,128]{4,3,2,1,0:T(8,128)(2,1)} collective-permute-done((bf16[8,2,16,16,128]{4,3,2,1,0:T(8,128)(2,1)}, bf16[8,2,16,16,128]{4,3,2,1,0:T(8,128)(2,1)}, u32[]{:S(2)}, u32[]{:S(2)}) %collective-permute-start.19) | collective-permute-done | bytes 1048608 | tf_op jit(solution)/shard_map/ppermute | solution.py:530
  192.6 5.7 %all-to-all-start.7 = ((bf16[8,2,16,16,128]{4,3,2,1,0:T(8,128)(2,1)}), bf16[8,2,16,16,128]{4,3,2,1,0:T(8,128)(2,1)S(1)}, u32[]{:S(2)}, u32[]{:S(2)}) async-start(bf16[8,2,16,16,128]{4,3,2,1,0:T(8,128)(2,1)} %fusion), calls=%async_computation.7 | async-start | bytes 2097152 | tf_op jit(solution)/shard_map/all_to_all | solution.py:533
  198.4 12.9 %collective-permute-done.refs_10_ = bf16[8,2,16,16,128]{4,3,2,1,0:T(8,128)(2,1)} collective-permute-done((bf16[8,2,16,16,128]{4,3,2,1,0:T(8,128)(2,1)S(1)}, bf16[8,2,16,16,128]{4,3,2,1,0:T(8,128)(2,1)}, u32[]{:S(2)}, u32[]{:S(2)}) %collective-permute-start) | collective-permute-done | bytes 1048608 | tf_op jit(solution)/shard_map/ppermute | solution.py:530
  216.1 13.9 %degrees.4 = (bf16[2,8,2,16,16,128]{5,4,3,2,1,0:T(8,128)(2,1)}, bf16[2,8,2,16,16,128]{5,4,3,2,1,0:T(8,128)(2,1)}) custom-call(s32[41]{0:T(128)} %concatenate.16.sc_ref, bf16[64,128,512]{2,1,0:T(8,128)(2,1)} %refs_7_.7, bf16[64,128,512]{2,1,0:T(8,128)(2,1)} %refs_7_.7, bf16[64,128,512]{2,1,0:T(8,128)(2,1)} %refs_7_.7, bf16[64,128,512]{2,1,0:T(8,128)(2,1)} %refs_7_.7, ...), custom_call_target="tpu_custom_call" | custom-call | flops 1207959552 | bytes 16777216 | tf_op jit(solution)/shard_map/degrees/pallas_call | solution.py:234
  230.6 11.3 %collective-permute-done.14 = bf16[8,2,16,16,128]{4,3,2,1,0:T(8,128)(2,1)} collective-permute-done((bf16[8,2,16,16,128]{4,3,2,1,0:T(8,128)(2,1)}, bf16[8,2,16,16,128]{4,3,2,1,0:T(8,128)(2,1)}, u32[]{:S(2)}, u32[]{:S(2)}) %collective-permute-start.14) | collective-permute-done | bytes 1048608 | tf_op jit(solution)/shard_map/ppermute | solution.py:530
  244.9 5.7 %all-to-all-start.5 = ((bf16[8,2,16,16,128]{4,3,2,1,0:T(8,128)(2,1)}), bf16[8,2,16,16,128]{4,3,2,1,0:T(8,128)(2,1)S(1)}, u32[]{:S(2)}, u32[]{:S(2)}) async-start(bf16[8,2,16,16,128]{4,3,2,1,0:T(8,128)(2,1)} %fusion.1), calls=%async_computation.5 | async-start | bytes 2097152 | tf_op jit(solution)/shard_map/all_to_all | solution.py:533
  252.7 24.4 %collective-permute-done.9 = bf16[8,2,16,16,128]{4,3,2,1,0:T(8,128)(2,1)S(1)} collective-permute-done((bf16[8,2,16,16,128]{4,3,2,1,0:T(8,128)(2,1)S(1)}, bf16[8,2,16,16,128]{4,3,2,1,0:T(8,128)(2,1)S(1)}, u32[]{:S(2)}, u32[]{:S(2)}) %collective-permute-start.9) | collective-permute-done | bytes 1048608 | tf_op jit(solution)/shard_map/ppermute | solution.py:530
  279.8 5.7 %all-to-all-start.3 = ((bf16[8,2,16,16,128]{4,3,2,1,0:T(8,128)(2,1)}), bf16[8,2,16,16,128]{4,3,2,1,0:T(8,128)(2,1)S(1)}, u32[]{:S(2)}, u32[]{:S(2)}) async-start(bf16[8,2,16,16,128]{4,3,2,1,0:T(8,128)(2,1)} %fusion.2), calls=%async_computation.3 | async-start | bytes 2097152 | tf_op jit(solution)/shard_map/all_to_all | solution.py:533
  287.9 22.7 %collective-permute-done.4 = bf16[8,2,16,16,128]{4,3,2,1,0:T(8,128)(2,1)S(1)} collective-permute-done((bf16[8,2,16,16,128]{4,3,2,1,0:T(8,128)(2,1)S(1)}, bf16[8,2,16,16,128]{4,3,2,1,0:T(8,128)(2,1)S(1)}, u32[]{:S(2)}, u32[]{:S(2)}) %collective-permute-start.4) | collective-permute-done | bytes 1048608 | tf_op jit(solution)/shard_map/ppermute | solution.py:530
  313.3 5.7 %all-to-all-start.1 = ((bf16[8,2,16,16,128]{4,3,2,1,0:T(8,128)(2,1)}), bf16[8,2,16,16,128]{4,3,2,1,0:T(8,128)(2,1)S(1)}, u32[]{:S(2)}, u32[]{:S(2)}) async-start(bf16[8,2,16,16,128]{4,3,2,1,0:T(8,128)(2,1)} %fusion.3), calls=%async_computation.1 | async-start | bytes 2097152 | tf_op jit(solution)/shard_map/all_to_all | solution.py:533
  319.0 18.9 %synthesis.2.refs_2_ = f32[64,2,16,1024]{3,2,1,0:T(8,128)} custom-call(bf16[256,16,128]{2,1,0:T(8,128)(2,1)} %bitcast.168, bf16[256,16,128]{2,1,0:T(8,128)(2,1)} %bitcast.167, bf16[256,16,128]{2,1,0:T(8,128)(2,1)} %bitcast.166, bf16[256,1024]{1,0:T(8,128)(2,1)} %get-tuple-element.50.refs_8_.refs_3_, bf16[256,1024]{1,0:T(8,128)(2,1)} %get-tuple-element.53.refs_8_.refs_4_, ...), custom_call_target="tpu_custom_call" | custom-call | flops 3221225472 | bytes 25165824 | tf_op jit(solution)/shard_map/synthesis/pallas_call | solution.py:380
  342.0 14.2 %synthesis.3 = (f32[2,2,4,1024,128]{4,3,2,1,0:T(8,128)S(1)}, f32[8,128]{1,0:T(8,128)S(1)}, f32[2,2,4,1024,128]{4,3,2,1,0:T(8,128)S(1)}, f32[2,2,4,1024,128]{4,3,2,1,0:T(8,128)S(1)}) custom-call(bf16[256,16,128]{2,1,0:T(8,128)(2,1)S(1)} %bitcast.143, bf16[256,1024]{1,0:T(8,128)(2,1)S(1)} %copy-done, f32[64,2,16,1024]{3,2,1,0:T(8,128)} %synthesis.2.refs_2_, ...), custom_call_target="tpu_custom_call" | custom-call | flops 1073741824 | bytes 33554432 | tf_op jit(solution)/shard_map/synthesis/pallas_call | solution.py:380
  370.5 12.3 %update.1 = (f32[64,2,16,1024]{3,2,1,0:T(8,128)}, f32[64,2,16,1024]{3,2,1,0:T(8,128)}, f32[64,2,16,1024]{3,2,1,0:T(8,128)}) custom-call(f32[8,128]{1,0:T(8,128)S(1)} %add.664.refs_0_, f32[8,128]{1,0:T(8,128)S(1)} %collective-permute-done.24.refs_1_, f32[8,128]{1,0:T(8,128)S(1)} %collective-permute-done.25.refs_2_, ...), custom_call_target="tpu_custom_call" | custom-call | flops 12582912 | bytes 33554432 | tf_op jit(solution)/shard_map/update/pallas_call | solution.py:439
  (109 shorter events, 74.8 us)
Async XLA Ops:
  54.8 38.4 %all-to-all-start.4 = ((bf16[8,2,16,16,128]{4,3,2,1,0:T(8,128)(2,1)}), bf16[8,2,16,16,128]{4,3,2,1,0:T(8,128)(2,1)S(1)}, u32[]{:S(2)}, u32[]{:S(2)}) async-start(bf16[8,2,16,16,128]{4,3,2,1,0:T(8,128)(2,1)} %bitcast.29), calls=%async_computation.4 | async-start | bytes 2097152 | tf_op jit(solution)/shard_map/all_to_all | solution.py:533
  58.4 25.2 %collective-permute-start.15 = (bf16[8,2,16,16,128]{4,3,2,1,0:T(8,128)(2,1)S(1)}, bf16[8,2,16,16,128]{4,3,2,1,0:T(8,128)(2,1)}, u32[]{:S(2)}, u32[]{:S(2)}) collective-permute-start(bf16[8,2,16,16,128]{4,3,2,1,0:T(8,128)(2,1)S(1)} %all_to_all.40.refs_9_), channel_id=1, source_target_pairs={{0,2},{1,3},{4,6},{5,7},{8,10},{9,11},{12,14},{13,15},{16,18},{17,... | collective-permute-start | bytes 3145736 | tf_op jit(solution)/shard_map/ppermute | solution.py:530
  62.7 48.9 %collective-permute-start.16 = (bf16[8,2,16,16,128]{4,3,2,1,0:T(8,128)(2,1)S(1)}, bf16[8,2,16,16,128]{4,3,2,1,0:T(8,128)(2,1)}, u32[]{:S(2)}, u32[]{:S(2)}) collective-permute-start(bf16[8,2,16,16,128]{4,3,2,1,0:T(8,128)(2,1)S(1)} %all_to_all.40.refs_9_), channel_id=1, source_target_pairs={{0,1},{1,0},{2,3},{3,2},{4,5},{5,4},{6,7},{7,6},{8,9},{9,8},{10,11... | collective-permute-start | bytes 3145736 | tf_op jit(solution)/shard_map/ppermute | solution.py:552
  83.6 28.1 %collective-permute-start.17 = (bf16[8,2,16,16,128]{4,3,2,1,0:T(8,128)(2,1)}, bf16[8,2,16,16,128]{4,3,2,1,0:T(8,128)(2,1)}, u32[]{:S(2)}, u32[]{:S(2)}) collective-permute-start(bf16[8,2,16,16,128]{4,3,2,1,0:T(8,128)(2,1)} %collective-permute-done.15.refs_10_), channel_id=1, source_target_pairs={{0,1},{1,0},{2,3},{3,2},{4,5},{5,4},{6,7},{7,6},{8,9},{9,8},{10,11... | collective-permute-start | bytes 3145736 | tf_op jit(solution)/shard_map/ppermute | solution.py:552
  93.2 33.0 %all-to-all-start.2 = ((bf16[8,2,16,16,128]{4,3,2,1,0:T(8,128)(2,1)}), bf16[8,2,16,16,128]{4,3,2,1,0:T(8,128)(2,1)S(1)}, u32[]{:S(2)}, u32[]{:S(2)}) async-start(bf16[8,2,16,16,128]{4,3,2,1,0:T(8,128)(2,1)} %bitcast.165), calls=%async_computation.2 | async-start | bytes 2097152 | tf_op jit(solution)/shard_map/all_to_all | solution.py:533
  99.0 27.3 %collective-permute-start.10 = (bf16[8,2,16,16,128]{4,3,2,1,0:T(8,128)(2,1)S(1)}, bf16[8,2,16,16,128]{4,3,2,1,0:T(8,128)(2,1)}, u32[]{:S(2)}, u32[]{:S(2)}) collective-permute-start(bf16[8,2,16,16,128]{4,3,2,1,0:T(8,128)(2,1)S(1)} %all-to-all-done.4.refs_9_), channel_id=1, source_target_pairs={{0,2},{1,3},{4,6},{5,7},{8,10},{9,11},{12,14},{13,15},{16,18},{17,... | collective-permute-start | bytes 3145736 | tf_op jit(solution)/shard_map/ppermute | solution.py:530
  125.5 32.7 %collective-permute-start.18 = (bf16[2,8,2,16,16,128]{5,4,3,2,1,0:T(8,128)(2,1)}, bf16[2,8,2,16,16,128]{5,4,3,2,1,0:T(8,128)(2,1)}, u32[]{:S(2)}, u32[]{:S(2)}) collective-permute-start(bf16[2,8,2,16,16,128]{5,4,3,2,1,0:T(8,128)(2,1)} %get-tuple-element.31), channel_id=1, source_target_pairs={{0,1},{1,0},{2,3},{3,2},{4,5},{5,4},{6,7},{7,6},{8,9},{9,8},{10,11... | collective-permute-start | bytes 6291464 | tf_op jit(solution)/shard_map/ppermute | solution.py:556
  125.6 9.6 %collective-permute-start.11 = (bf16[8,2,16,16,128]{4,3,2,1,0:T(8,128)(2,1)S(1)}, bf16[8,2,16,16,128]{4,3,2,1,0:T(8,128)(2,1)}, u32[]{:S(2)}, u32[]{:S(2)}) collective-permute-start(bf16[8,2,16,16,128]{4,3,2,1,0:T(8,128)(2,1)S(1)} %all-to-all-done.4.refs_9_), channel_id=1, source_target_pairs={{0,1},{1,0},{2,3},{3,2},{4,5},{5,4},{6,7},{7,6},{8,9},{9,8},{10,11... | collective-permute-start | bytes 3145736 | tf_op jit(solution)/shard_map/ppermute | solution.py:552
  126.3 36.1 %all-to-all-start = ((bf16[8,2,16,16,128]{4,3,2,1,0:T(8,128)(2,1)}), bf16[8,2,16,16,128]{4,3,2,1,0:T(8,128)(2,1)S(1)}, u32[]{:S(2)}, u32[]{:S(2)}) async-start(bf16[8,2,16,16,128]{4,3,2,1,0:T(8,128)(2,1)} %bitcast.169), calls=%async_computation | async-start | bytes 2097152 | tf_op jit(solution)/shard_map/all_to_all | solution.py:533
  132.2 26.1 %collective-permute-start.5 = (bf16[8,2,16,16,128]{4,3,2,1,0:T(8,128)(2,1)S(1)}, bf16[8,2,16,16,128]{4,3,2,1,0:T(8,128)(2,1)}, u32[]{:S(2)}, u32[]{:S(2)}) collective-permute-start(bf16[8,2,16,16,128]{4,3,2,1,0:T(8,128)(2,1)S(1)} %all-to-all-done.2.refs_9_), channel_id=1, source_target_pairs={{0,2},{2,0},{1,3},{3,1},{4,6},{6,4},{5,7},{7,5},{8,10},{10,8},{9,1... | collective-permute-start | bytes 3145736 | tf_op jit(solution)/shard_map/ppermute | solution.py:530
  149.0 62.3 %collective-permute-start.13 = (bf16[2,8,2,16,16,128]{5,4,3,2,1,0:T(8,128)(2,1)}, bf16[2,8,2,16,16,128]{5,4,3,2,1,0:T(8,128)(2,1)}, u32[]{:S(2)}, u32[]{:S(2)}) collective-permute-start(bf16[2,8,2,16,16,128]{5,4,3,2,1,0:T(8,128)(2,1)} %get-tuple-element.28), channel_id=1, source_target_pairs={{0,1},{1,0},{2,3},{3,2},{4,5},{5,4},{6,7},{7,6},{8,9},{9,8},{10,11... | collective-permute-start | bytes 6291464 | tf_op jit(solution)/shard_map/ppermute | solution.py:556
  149.1 17.6 %collective-permute-start.6 = (bf16[8,2,16,16,128]{4,3,2,1,0:T(8,128)(2,1)S(1)}, bf16[8,2,16,16,128]{4,3,2,1,0:T(8,128)(2,1)S(1)}, u32[]{:S(2)}, u32[]{:S(2)}) collective-permute-start(bf16[8,2,16,16,128]{4,3,2,1,0:T(8,128)(2,1)S(1)} %all-to-all-done.2.refs_9_), channel_id=1, source_target_pairs={{0,1},{1,0},{2,3},{3,2},{4,5},{5,4},{6,7},{7,6},{8,9},{9,8},{10,11... | collective-permute-start | bytes 3145736 | tf_op jit(solution)/shard_map/ppermute | solution.py:552
  161.1 28.2 %collective-permute-start.19 = (bf16[8,2,16,16,128]{4,3,2,1,0:T(8,128)(2,1)}, bf16[8,2,16,16,128]{4,3,2,1,0:T(8,128)(2,1)}, u32[]{:S(2)}, u32[]{:S(2)}) collective-permute-start(bf16[8,2,16,16,128]{4,3,2,1,0:T(8,128)(2,1)} %fusion.35), channel_id=1, source_target_pairs={{2,0},{3,1},{6,4},{7,5},{10,8},{11,9},{14,12},{15,13},{18,16},{19,... | collective-permute-start | bytes 3145736 | tf_op jit(solution)/shard_map/ppermute | solution.py:530
  162.4 48.9 %collective-permute-start = (bf16[8,2,16,16,128]{4,3,2,1,0:T(8,128)(2,1)S(1)}, bf16[8,2,16,16,128]{4,3,2,1,0:T(8,128)(2,1)}, u32[]{:S(2)}, u32[]{:S(2)}) collective-permute-start(bf16[8,2,16,16,128]{4,3,2,1,0:T(8,128)(2,1)S(1)} %all-to-all-done.refs_9_), channel_id=1, source_target_pairs={{0,2},{2,0},{1,3},{3,1},{4,6},{6,4},{5,7},{7,5},{8,10},{10,8},{9,1... | collective-permute-start | bytes 3145736 | tf_op jit(solution)/shard_map/ppermute | solution.py:530
  181.5 69.1 %collective-permute-start.8 = (bf16[2,8,2,16,16,128]{5,4,3,2,1,0:T(8,128)(2,1)}, bf16[2,8,2,16,16,128]{5,4,3,2,1,0:T(8,128)(2,1)}, u32[]{:S(2)}, u32[]{:S(2)}) collective-permute-start(bf16[2,8,2,16,16,128]{5,4,3,2,1,0:T(8,128)(2,1)} %get-tuple-element.25), channel_id=1, source_target_pairs={{0,1},{1,0},{2,3},{3,2},{4,5},{5,4},{6,7},{7,6},{8,9},{9,8},{10,11... | collective-permute-start | bytes 6291464 | tf_op jit(solution)/shard_map/ppermute | solution.py:556
  192.6 52.3 %all-to-all-start.7 = ((bf16[8,2,16,16,128]{4,3,2,1,0:T(8,128)(2,1)}), bf16[8,2,16,16,128]{4,3,2,1,0:T(8,128)(2,1)S(1)}, u32[]{:S(2)}, u32[]{:S(2)}) async-start(bf16[8,2,16,16,128]{4,3,2,1,0:T(8,128)(2,1)} %fusion), calls=%async_computation.7 | async-start | bytes 2097152 | tf_op jit(solution)/shard_map/all_to_all | solution.py:533
  198.3 17.8 %collective-permute-start.1 = (bf16[8,2,16,16,128]{4,3,2,1,0:T(8,128)(2,1)S(1)}, bf16[8,2,16,16,128]{4,3,2,1,0:T(8,128)(2,1)}, u32[]{:S(2)}, u32[]{:S(2)}) collective-permute-start(bf16[8,2,16,16,128]{4,3,2,1,0:T(8,128)(2,1)S(1)} %all-to-all-done.refs_9_), channel_id=1, source_target_pairs={{0,1},{1,0},{2,3},{3,2},{4,5},{5,4},{6,7},{7,6},{8,9},{9,8},{10,11... | collective-permute-start | bytes 3145736 | tf_op jit(solution)/shard_map/ppermute | solution.py:552
  214.1 27.8 %collective-permute-start.14 = (bf16[8,2,16,16,128]{4,3,2,1,0:T(8,128)(2,1)}, bf16[8,2,16,16,128]{4,3,2,1,0:T(8,128)(2,1)}, u32[]{:S(2)}, u32[]{:S(2)}) collective-permute-start(bf16[8,2,16,16,128]{4,3,2,1,0:T(8,128)(2,1)} %fusion.33), channel_id=1, source_target_pairs={{2,0},{3,1},{6,4},{7,5},{10,8},{11,9},{14,12},{15,13},{18,16},{19,... | collective-permute-start | bytes 3145736 | tf_op jit(solution)/shard_map/ppermute | solution.py:530
  230.1 55.5 %collective-permute-start.3 = (bf16[2,8,2,16,16,128]{5,4,3,2,1,0:T(8,128)(2,1)}, bf16[2,8,2,16,16,128]{5,4,3,2,1,0:T(8,128)(2,1)}, u32[]{:S(2)}, u32[]{:S(2)}) collective-permute-start(bf16[2,8,2,16,16,128]{5,4,3,2,1,0:T(8,128)(2,1)} %get-tuple-element.23), channel_id=1, source_target_pairs={{0,1},{1,0},{2,3},{3,2},{4,5},{5,4},{6,7},{7,6},{8,9},{9,8},{10,11... | collective-permute-start | bytes 6291464 | tf_op jit(solution)/shard_map/ppermute | solution.py:556
  244.9 34.9 %all-to-all-start.5 = ((bf16[8,2,16,16,128]{4,3,2,1,0:T(8,128)(2,1)}), bf16[8,2,16,16,128]{4,3,2,1,0:T(8,128)(2,1)S(1)}, u32[]{:S(2)}, u32[]{:S(2)}) async-start(bf16[8,2,16,16,128]{4,3,2,1,0:T(8,128)(2,1)} %fusion.1), calls=%async_computation.5 | async-start | bytes 2097152 | tf_op jit(solution)/shard_map/all_to_all | solution.py:533
  252.6 24.5 %collective-permute-start.9 = (bf16[8,2,16,16,128]{4,3,2,1,0:T(8,128)(2,1)S(1)}, bf16[8,2,16,16,128]{4,3,2,1,0:T(8,128)(2,1)S(1)}, u32[]{:S(2)}, u32[]{:S(2)}) collective-permute-start(bf16[8,2,16,16,128]{4,3,2,1,0:T(8,128)(2,1)S(1)} %fusion.31), channel_id=1, source_target_pairs={{0,2},{2,0},{1,3},{3,1},{4,6},{6,4},{5,7},{7,5},{8,10},{10,8},{9,1... | collective-permute-start | bytes 3145736 | tf_op jit(solution)/shard_map/ppermute | solution.py:530
  279.8 33.5 %all-to-all-start.3 = ((bf16[8,2,16,16,128]{4,3,2,1,0:T(8,128)(2,1)}), bf16[8,2,16,16,128]{4,3,2,1,0:T(8,128)(2,1)S(1)}, u32[]{:S(2)}, u32[]{:S(2)}) async-start(bf16[8,2,16,16,128]{4,3,2,1,0:T(8,128)(2,1)} %fusion.2), calls=%async_computation.3 | async-start | bytes 2097152 | tf_op jit(solution)/shard_map/all_to_all | solution.py:533
  287.5 23.1 %collective-permute-start.4 = (bf16[8,2,16,16,128]{4,3,2,1,0:T(8,128)(2,1)S(1)}, bf16[8,2,16,16,128]{4,3,2,1,0:T(8,128)(2,1)S(1)}, u32[]{:S(2)}, u32[]{:S(2)}) collective-permute-start(bf16[8,2,16,16,128]{4,3,2,1,0:T(8,128)(2,1)S(1)} %fusion.29), channel_id=1, source_target_pairs={{0,2},{2,0},{1,3},{3,1},{4,6},{6,4},{5,7},{7,5},{8,10},{10,8},{9,1... | collective-permute-start | bytes 3145736 | tf_op jit(solution)/shard_map/ppermute | solution.py:530
  313.3 28.7 %all-to-all-start.1 = ((bf16[8,2,16,16,128]{4,3,2,1,0:T(8,128)(2,1)}), bf16[8,2,16,16,128]{4,3,2,1,0:T(8,128)(2,1)S(1)}, u32[]{:S(2)}, u32[]{:S(2)}) async-start(bf16[8,2,16,16,128]{4,3,2,1,0:T(8,128)(2,1)} %fusion.3), calls=%async_computation.1 | async-start | bytes 2097152 | tf_op jit(solution)/shard_map/all_to_all | solution.py:533
  (22 other events, 299.6 us)

commit v2 on v1

--- a/solution.py
+++ b/solution.py
@@ -11,6 +11,7 @@
 LANES = 128
 PACK = 16
 PLAN = ((0, 0), (1, 0), (1, 1), (0, 1))
+TRIPS = ((0,), (1,), (2, 3))
 CHUNKS = len(PLAN)
 BF = jnp.bfloat16
 F32 = jnp.float32
@@ -70,7 +71,7 @@
     return lax.broadcasted_iota(jnp.int32, shape, len(shape) - 1) < LANES // 2
 
 
-def analysis_call(direction4, tables):
+def analysis_call(direction4, tables, groups, nb):
     cycles, lo_n, hi_n, length = direction4.shape
     cols = tables[0].shape[0]
     n_tab = len(tables)
@@ -81,7 +82,7 @@
     def kernel(*refs):
         x_refs = refs[:parts_n]
         tab_refs = refs[parts_n : parts_n + n_tab]
-        o_refs = refs[parts_n + n_tab : parts_n + 2 * n_tab]
+        o_refs = refs[parts_n + n_tab : -1]
         s_ref = refs[-1]
         h = pl.program_id(0)
         flat = [ref.reshape(cycles * lo_n * sub, LANES) for ref in x_refs]
@@ -107,20 +108,24 @@
 
         @pl.when(h == steps - 1)
         def _():
-            for n in range(n_tab):
-                o_refs[n][...] = s_ref[n].reshape(cols, hi_n, LANES).astype(BF)
-
-    out = jax.ShapeDtypeStruct((cols, hi_n, LANES), BF)
+            n = 0
+            for ref, count in zip(o_refs, groups):
+                for slot in range(count):
+                    rows = s_ref[n].reshape(nb, cols // nb, hi_n, LANES)
+                    ref[:, slot] = rows.astype(BF)
+                    n += 1
+
+    shapes = [(nb, count, cols // nb, hi_n, LANES) for count in groups]
     return pl.pallas_call(
         kernel,
-        out_shape=(out,) * n_tab,
+        out_shape=tuple(jax.ShapeDtypeStruct(shape, BF) for shape in shapes),
         grid=(steps,),
         in_specs=[
             pl.BlockSpec((cycles, lo_n, sub, LANES), lambda h, p=p: (0, 0, h, p))
             for p in range(parts_n)
         ]
         + [pl.BlockSpec((cols, length), lambda h: (0, 0))] * n_tab,
-        out_specs=(pl.BlockSpec((cols, hi_n, LANES), lambda h: (0, 0, 0)),) * n_tab,
+        out_specs=tuple(pl.BlockSpec(shape, lambda h: (0,) * 5) for shape in shapes),
         scratch_shapes=[pltpu.VMEM((n_tab, cols * hi_n, LANES), F32)],
         compiler_params=pltpu.CompilerParams(vmem_limit_bytes=60 << 20),
         cost_estimate=pl.CostEstimate(
@@ -280,7 +285,7 @@
     jb = 512
     batch = 4
     last = previous is not None
-    n_grid = 3 if last else 2
+    n_grid = 4 if last else 2
 
     def kernel(*refs):
         rec_refs = refs[:n_tab]
@@ -292,7 +297,27 @@
         h, j = pl.program_id(0), pl.program_id(1)
         if last:
             p_ref = o_ref.at[h, j]
-            d_ref, r_ref = (refs[2 * n_tab + n_grid + n].at[h, j] for n in (2, 3))
+            near_refs = refs[2 * n_tab + n_grid + 2 : 2 * n_tab + n_grid + 5]
+            d_ref, r_ref = (ref.at[h, j] for ref in near_refs[:2])
+            sem = refs[-2]
+
+            def fetch(n, hh, jj):
+                source = grid_refs[1 + n].at[
+                    :, :, hh * sub : (hh + 1) * sub, jj * jb : (jj + 1) * jb
+                ]
+                return pltpu.make_async_copy(source, near_refs[n].at[hh, jj], sem.at[n, hh, jj])
+
+            spots = [(hh, jj) for hh in range(hi_n // sub) for jj in range(length // jb)]
+
+            @pl.when((h == 0) & (j == 0))
+            def _():
+                for n in (0, 1):
+                    fetch(n, 0, 0).start()
+                for spot in spots[1:]:
+                    for n in (0, 1):
+                        fetch(n, *spot).start()
+                for spot in spots:
+                    fetch(2, *spot).start()
         else:
             p_ref = refs[-2]
 
@@ -330,6 +355,19 @@
             return carry
 
         lax.fori_loop(0, sub // batch, some, 0)
+        if last:
+            for hh, jj in spots:
+
+                @pl.when((h == hh) & (j == jj))
+                def _():
+                    for n in (0, 1):
+                        fetch(n, hh, jj).wait()
+
+            @pl.when((h == spots[-1][0]) & (j == spots[-1][1]))
+            def _():
+                for spot in spots:
+                    fetch(2, *spot).wait()
+
         group = 8
 
         def finish(i, carry):
@@ -342,12 +380,11 @@
                 p = p_ref[part, rows, :].reshape(group, lo_n, sub, LANES)
                 if last:
                     p = p + grid_refs[0][block, :, :, lanes]
-                    d = grid_refs[1][block, :, :, lanes]
-                    r = grid_refs[2][block, :, :, lanes]
+                    d = d_ref[block, :, :, lanes]
+                    r = r_ref[block, :, :, lanes]
                     for n, term in enumerate((r * r, d * p, r * p, p * p)):
                         carry[n] = carry[n] + jnp.sum(term, axis=(0, 1))
-                    for ref, v in ((p_ref, p), (d_ref, d), (r_ref, r)):
-                        ref[part, rows, :] = v.reshape(span, LANES)
+                    p_ref[part, rows, :] = p.reshape(span, LANES)
                 else:
                     p = p + grid_refs[0][block, :, :, lanes] * grid_refs[1][block, :, :, lanes]
                     o_ref[block, :, :, lanes] = p
@@ -365,14 +402,16 @@
     in_specs = (
         [pl.BlockSpec((cols, hi_n, LANES), lambda h, j: (0, 0, 0))] * n_tab
         + [pl.BlockSpec((cols, jb), lambda h, j: (0, j))] * n_tab
-        + [grid_block] * n_grid
+        + ([grid_block] + [pl.BlockSpec(memory_space=pltpu.HBM)] * 3 if last else [grid_block] * 2)
     )
     tile_rows = cycles * lo_n * sub
     if last:
         held = pltpu.VMEM((hi_n // sub, length // jb, jb // LANES, tile_rows, LANES), F32)
         whole = pl.BlockSpec(memory_space=pltpu.VMEM)
-        out_shape = [held, jax.ShapeDtypeStruct((sub, LANES), F32), held, held]
-        out_specs = [whole, pl.BlockSpec((sub, LANES), lambda h, j: (0, 0)), whole, whole]
+        steps = (hi_n // sub, length // jb)
+        near = pltpu.VMEM(steps + (cycles, lo_n, sub, jb), F32)
+        out_shape = [held, jax.ShapeDtypeStruct((sub, LANES), F32)] + [near] * 3
+        out_specs = [whole, pl.BlockSpec((sub, LANES), lambda h, j: (0, 0))] + [whole] * 3
     else:
         out_shape = [jax.ShapeDtypeStruct((cycles, lo_n, hi_n, length), F32)]
         out_specs = [grid_block]
@@ -383,9 +422,13 @@
         grid=(hi_n // sub, length // jb),
         in_specs=in_specs,
         out_specs=tuple(out_specs),
-        scratch_shapes=([] if last else [pltpu.VMEM((jb // LANES, tile_rows, LANES), F32)])
+        scratch_shapes=[
+            pltpu.SemaphoreType.DMA((3, hi_n // sub, length // jb))
+            if last
+            else pltpu.VMEM((jb // LANES, tile_rows, LANES), F32)
+        ]
         + [pltpu.VMEM((n_tab * cols * hi_n, LANES), F32)],
-        compiler_params=pltpu.CompilerParams(vmem_limit_bytes=(24 << 20) if last else (60 << 20)),
+        compiler_params=pltpu.CompilerParams(vmem_limit_bytes=(16 << 20) if last else (60 << 20)),
         cost_estimate=pl.CostEstimate(
             flops=2 * n_tab * cols * LANES * hi_n * length,
             bytes_accessed=4 * cycles * lo_n * hi_n * length * (n_grid + 1),
@@ -395,17 +438,17 @@
     )(*received, *tables, *grids)
 
 
-def update_call(sums, solution4, held):
-    cycles, lo_n, hi_n, length = solution4.shape
-    _, steps_j, parts, _, _ = held[0].shape
-    sub, jb = hi_n // held[0].shape[0], length // steps_j
+def update_call(sums, held):
+    steps_h, steps_j, cycles, lo_n, sub, jb = held[1].shape
+    parts = jb // LANES
+    shape4 = (cycles, lo_n, steps_h * sub, steps_j * jb)
     group = 8
     span = group * lo_n * sub
 
     n_sums = len(sums)
 
     def kernel(*refs):
-        x_ref, p_ref, r_ref, d_ref, xo_ref, ro_ref, do_ref = refs[n_sums:]
+        p_ref, d_ref, r_ref, x_ref, xo_ref, ro_ref, do_ref = refs[n_sums:]
         h, j = pl.program_id(0), pl.program_id(1)
         total = refs[0][...]
         for ref in refs[1:n_sums]:
@@ -422,11 +465,9 @@
             rows = pl.ds(pl.multiple_of(i * span, span), span)
             for part in range(parts):
                 lanes = slice(part * LANES, (part + 1) * LANES)
-                p, r, d = (
-                    ref[h, j, part, rows, :].reshape(group, lo_n, sub, LANES)
-                    for ref in (p_ref, r_ref, d_ref)
-                )
-                xo_ref[block, :, :, lanes] = x_ref[block, :, :, lanes] + step * d
+                p = p_ref[h, j, part, rows, :].reshape(group, lo_n, sub, LANES)
+                d, r, x = (ref[h, j, block, :, :, lanes] for ref in (d_ref, r_ref, x_ref))
+                xo_ref[block, :, :, lanes] = x + step * d
                 r = r - step * p
                 ro_ref[block, :, :, lanes] = r
                 do_ref[block, :, :, lanes] = r + ratio * d
@@ -435,21 +476,20 @@
         lax.fori_loop(0, cycles // group, some, 0)
 
     spec = pl.BlockSpec((cycles, lo_n, sub, jb), lambda h, j: (0, 0, h, j))
-    size = solution4.size
+    size = math.prod(shape4)
     return pl.pallas_call(
         kernel,
-        out_shape=(jax.ShapeDtypeStruct(solution4.shape, F32),) * 3,
-        grid=(hi_n // sub, steps_j),
+        out_shape=(jax.ShapeDtypeStruct(shape4, F32),) * 3,
+        grid=(steps_h, steps_j),
         in_specs=[pl.BlockSpec(sums[0].shape, lambda h, j: (0, 0))] * n_sums
-        + [spec]
-        + [pl.BlockSpec(memory_space=pltpu.VMEM)] * 3,
+        + [pl.BlockSpec(memory_space=pltpu.VMEM)] * 4,
         out_specs=(spec,) * 3,
-        compiler_params=pltpu.CompilerParams(vmem_limit_bytes=24 << 20),
+        compiler_params=pltpu.CompilerParams(vmem_limit_bytes=16 << 20),
         cost_estimate=pl.CostEstimate(
-            flops=6 * size, bytes_accessed=16 * size, transcendentals=0
+            flops=6 * size, bytes_accessed=12 * size, transcendentals=0
         ),
         name="update",
-    )(*sums, solution4, *(pltpu.with_memory_space_constraint(v, pltpu.VMEM) for v in held))
+    )(*sums, *(pltpu.with_memory_space_constraint(v, pltpu.VMEM) for v in held))
 
 
 def add_call(values):
@@ -508,16 +548,19 @@
     own_rows = jnp.stack([slots + flip, slots + half - flip])
     own_orders = jnp.stack([jnp.min(own, axis=0), jnp.max(own, axis=0)])
     shape4 = (cycles, lo_n, hi_n, longitude)
-    direction4, noise4, residual4 = (v.reshape(shape4) for v in (direction, noise_var, residual))
+    fields = (solution, residual, direction, noise_var)
+    solution4, residual4, direction4, noise4 = (v.reshape(shape4) for v in fields)
     quarter = (longitude // 4) * 3
 
-    def table_of(chunk):
+    def table_of(chunk, grouped):
         high, start = PLAN[chunk]
         orders = grouped[high][:, start * chunk_n : (start + 1) * chunk_n]
         points = jnp.arange(longitude, dtype=jnp.int32)
         turn = jnp.arange(2, dtype=jnp.int32) * quarter
         phases = orders[:, None, :, None] * points + turn[None, :, None, None]
-        return sine_table(phases % longitude, longitude).astype(BF).reshape(cols, longitude)
+        whole = longitude & (longitude - 1) == 0
+        phases = phases & (longitude - 1) if whole else phases % longitude
+        return sine_table(phases, longitude).astype(BF).reshape(cols, longitude)
 
     forth = [jnp.mod(x_i - s, n_x) * n_core + (core_i + o) % n_core for o in range(2) for s in range(n_x)]
     back = [jnp.mod(x_i + s, n_x) * n_core + (core_i + o) % n_core for o in range(2) for s in range(n_x)]
@@ -532,12 +575,18 @@
     def across(v):
         return lax.all_to_all(v, "blk", split_axis=0, concat_axis=0, tiled=True)
 
-    tables = [table_of(0)]
-    spectra = list(analysis_call(direction4, tables))
+    tables = [table_of(0, grouped)]
+    spectra = list(analysis_call(direction4, tables, (1,), nb))
     piece = (nb, 2, chunk_n, hi_n, LANES)
-    tables += [table_of(g) for g in range(1, CHUNKS)]
-    spectra += list(analysis_call(direction4, tables[1:]))
+    later, spectra[0] = lax.optimization_barrier((grouped, spectra[0]))
+    tables += [table_of(g, later) for g in range(1, CHUNKS)]
+    counts = tuple(len(trip) for trip in TRIPS[1:])
+    spectra += list(analysis_call(direction4, tables[1:], counts, nb))
     temporal_narrow = temporal.astype(BF)
+    arrived = []
+    for n, trip in enumerate(TRIPS):
+        moved = across(spectra[n])
+        arrived += [moved[:, slot].reshape(piece) for slot in range(len(trip))]
     received = []
     for g, (high, start) in enumerate(PLAN):
 
@@ -547,7 +596,7 @@
         def backward(source, target):
             return source > 0 or not high
 
-        mine = across(spectra[g].reshape(piece))
+        mine = arrived[g]
         own = [mine] + [shift(mine, s, forward) for s in range(1, n_x)]
         pieces = own + [lax.ppermute(v, "core", swap) for v in own]
         span = slice(start * chunk_n, (start + 1) * chunk_n)
@@ -564,11 +613,11 @@
         received.append(across(total).reshape(cols, hi_n, LANES))
     scale = 2.0 / longitude
     (partial,) = synthesis_call(received[:-1], tables[:-1], None, (noise4, direction4), scale)
-    product, sums, near_d, near_r = synthesis_call(
-        received[-1:], tables[-1:], partial, (direction4, residual4), scale
+    product, sums, *near = synthesis_call(
+        received[-1:], tables[-1:], partial, (direction4, residual4, solution4), scale
     )
     sums = sum_parts(sums, nb, n_x, n_core)
-    out = update_call(sums, solution.reshape(shape4), (product, near_r, near_d))
+    out = update_call(sums, (product, *near))
     return tuple(v.reshape(direction.shape) for v in out)
 
 

time: 384 us -> 384 us (level)
  waiting for transfers between devices: 123 us -> 132 us
  starting transfers between devices: 63.1 us -> 57.8 us
    all_to_all x7 -> x6, waiting for transfers between devices: 4.09 us -> 11.9 us  [across(): return lax.all_to_all(v, 'blk', split_axis=0, concat_axis=0, tiled=True)]
    all_to_all x7 -> x6, starting transfers between devices: 38.1 us -> 33.8 us  [across(): return lax.all_to_all(v, 'blk', split_axis=0, concat_axis=0, tiled=True)]
  transfers between devices with their start and end apart: 34 -> 33, of which waited for: 16 -> 16; matrix products, arithmetic and copies ran while one was open for 8% -> 9% of each run, Pallas kernels for 22% -> 23%
where the time goes in v2:
time: 384 us; the launch traced here: 383 us
  waiting for transfers between devices  132 us (34%)
  Pallas kernels  124 us (32%)
  starting transfers between devices  57.8 us (15%)
  other arithmetic  32.5 us (8%)
  blocking collectives  29.7 us (8%)
  local copies, waits for them, and re-layouts  6.48 us (2%)
    ppermute x8, waiting for transfers between devices, shift(): return lax.ppermute(v, 'x', [pair for pair in pairs if keep(*pair)])  110 us
    pallas_call x4, Pallas kernels, degree_call(): pl.pallas_call(kernel, out_shape=(out_shape, out_shape), grid_spec=pltpu....  55.6 us
    pallas_call x2, Pallas kernels, synthesis_call(): pl.pallas_call(kernel, out_shape=tuple(out_shape), grid=(hi_n // sub, len...  34.7 us
    all_to_all x6, starting transfers between devices, across(): return lax.all_to_all(v, 'blk', split_axis=0, concat_axis=0, tiled=True)  33.8 us
    all_to_all x1, blocking collectives, across(): return lax.all_to_all(v, 'blk', split_axis=0, concat_axis=0, tiled=True)  29.7 us
    pallas_call x2, Pallas kernels, analysis_call(): pl.pallas_call(kernel, out_shape=tuple((jax.ShapeDtypeStruct(shape, BF) f...  23.9 us
    ppermute x8, starting transfers between devices, shift(): return lax.ppermute(v, 'x', [pair for pair in pairs if keep(*pair)])  18 us
    all_to_all x6, waiting for transfers between devices, across(): return lax.all_to_all(v, 'blk', split_axis=0, concat_axis=0, tiled=True)  11.9 us
  transfers between devices with their start and end apart: 33, of which 16 were waited for; matrix products, arithmetic and copies ran while one was open for 9% of the time, Pallas kernels for 23%

profile of v2, /device:TPU:0, one launch (start us, length us, event | category | flops | bytes accessed | tf_op | source)
XLA Modules:
  0.0 383.2 jit_solution(8315187107904898160)
XLA Ops:
  3.4 9.7 %analysis.2 = bf16[8,1,32,16,128]{4,3,2,1,0:T(8,128)(2,1)} custom-call(f32[64,2,16,1024]{3,2,1,0:T(8,128)} %bitcast.279, f32[64,2,16,1024]{3,2,1,0:T(8,128)} %bitcast.280, f32[64,2,16,1024]{3,2,1,0:T(8,128)} %bitcast.281, f32[64,2,16,1024]{3,2,1,0:T(8,128)} %bitcast.282, f32[64,2,16,1024]{3,2,1,0:T(8,128)} %bitcast.283, f32[64,2,16,1024]{3,2,1,0:T(8,128)} %bitcast.284, ...), custom_call_target="tpu_custom_call" | custom-call | flops 1073741824 | bytes 8912896 | tf_op jit(solution)/shard_map/analysis/pallas_call | solution.py:119
  13.0 7.3 %all-to-all-start.2 = ((bf16[8,1,32,16,128]{4,3,2,1,0:T(8,128)(2,1)}), bf16[8,1,32,16,128]{4,3,2,1,0:T(8,128)(2,1)S(1)}, u32[]{:S(2)}, u32[]{:S(2)}) async-start(bf16[8,1,32,16,128]{4,3,2,1,0:T(8,128)(2,1)} %analysis.2), calls=%async_computation.2 | async-start | bytes 2097152 | tf_op jit(solution)/shard_map/all_to_all | solution.py:576
  24.0 14.2 %analysis.3 = (bf16[8,1,32,16,128]{4,3,2,1,0:T(8,128)(2,1)}, bf16[8,2,32,16,128]{4,3,2,1,0:T(8,128)(2,1)}) custom-call(f32[64,2,16,1024]{3,2,1,0:T(8,128)} %bitcast.287, f32[64,2,16,1024]{3,2,1,0:T(8,128)} %bitcast.288, f32[64,2,16,1024]{3,2,1,0:T(8,128)} %bitcast.289, f32[64,2,16,1024]{3,2,1,0:T(8,128)} %bitcast.290, f32[64,2,16,1024]{3,2,1,0:T(8,128)} %bitcast.291, ...), custom_call_target="tpu_custom_call" | custom-call | flops 3221225472 | bytes 9961472 | tf_op jit(solution)/shard_map/analysis/pallas_call | solution.py:119
  38.3 7.8 %all-to-all-done.2 = bf16[8,1,32,16,128]{4,3,2,1,0:T(8,128)(2,1)S(1)} async-done(((bf16[8,1,32,16,128]{4,3,2,1,0:T(8,128)(2,1)}), bf16[8,1,32,16,128]{4,3,2,1,0:T(8,128)(2,1)S(1)}, u32[]{:S(2)}, u32[]{:S(2)}) %all-to-all-start.2) | async-done | bytes 1048608 | tf_op jit(solution)/shard_map/all_to_all | solution.py:576
  46.1 29.7 %all_to_all.35 = bf16[8,1,32,16,128]{4,3,2,1,0:T(8,128)(2,1)} all-to-all(bf16[8,1,32,16,128]{4,3,2,1,0:T(8,128)(2,1)} %get-tuple-element.30), channel_id=1, replica_groups=mesh['blk'=8,'x'=2,'core'=2] {'blk'}, dimensions={0} | all-to-all | bytes 2097152 | tf_op jit(solution)/shard_map/all_to_all | solution.py:576
  83.8 21.0 %collective-permute-done.10.refs_10_ = bf16[8,2,16,16,128]{4,3,2,1,0:T(8,128)(2,1)} collective-permute-done((bf16[8,2,16,16,128]{4,3,2,1,0:T(8,128)(2,1)}, bf16[8,2,16,16,128]{4,3,2,1,0:T(8,128)(2,1)}, u32[]{:S(2)}, u32[]{:S(2)}) %collective-permute-start.10) | collective-permute-done | bytes 1048608 | tf_op jit(solution)/shard_map/ppermute | solution.py:573
  107.3 6.4 %convert_element_type.187.refs_8_ = bf16[128,128,128]{2,1,0:T(8,128)(2,1)} convert(f32[128,128,128]{2,1,0:T(8,128)} %param.12) | non-fusion elementwise | flops 2097152 | bytes 12582912 | tf_op jit(solution)/shard_map/convert_element_type | solution.py:585
  114.4 13.9 %degrees.6 = (bf16[2,8,2,16,16,128]{5,4,3,2,1,0:T(8,128)(2,1)}, bf16[2,8,2,16,16,128]{5,4,3,2,1,0:T(8,128)(2,1)}) custom-call(s32[41]{0:T(128)} %concatenate.18.sc_ref, bf16[64,128,512]{2,1,0:T(8,128)(2,1)} %refs_7_.7, bf16[64,128,512]{2,1,0:T(8,128)(2,1)} %refs_7_.7, bf16[64,128,512]{2,1,0:T(8,128)(2,1)} %refs_7_.7, bf16[64,128,512]{2,1,0:T(8,128)(2,1)} %refs_7_.7, ...), custom_call_target="tpu_custom_call" | custom-call | flops 1207959552 | bytes 16777216 | tf_op jit(solution)/shard_map/degrees/pallas_call | solution.py:239
  138.3 14.0 %degrees.5 = (bf16[2,8,2,16,16,128]{5,4,3,2,1,0:T(8,128)(2,1)}, bf16[2,8,2,16,16,128]{5,4,3,2,1,0:T(8,128)(2,1)}) custom-call(s32[41]{0:T(128)} %concatenate.17.sc_ref, bf16[64,128,512]{2,1,0:T(8,128)(2,1)} %refs_7_.7, bf16[64,128,512]{2,1,0:T(8,128)(2,1)} %refs_7_.7, bf16[64,128,512]{2,1,0:T(8,128)(2,1)} %refs_7_.7, bf16[64,128,512]{2,1,0:T(8,128)(2,1)} %refs_7_.7, ...), custom_call_target="tpu_custom_call" | custom-call | flops 1207959552 | bytes 16777216 | tf_op jit(solution)/shard_map/degrees/pallas_call | solution.py:239
  152.8 7.1 %collective-permute-done.15.refs_10_ = bf16[8,2,16,16,128]{4,3,2,1,0:T(8,128)(2,1)} collective-permute-done((bf16[8,2,16,16,128]{4,3,2,1,0:T(8,128)(2,1)}, bf16[8,2,16,16,128]{4,3,2,1,0:T(8,128)(2,1)}, u32[]{:S(2)}, u32[]{:S(2)}) %collective-permute-start.15) | collective-permute-done | bytes 1048608 | tf_op jit(solution)/shard_map/ppermute | solution.py:573
  167.9 13.9 %degrees.7 = (bf16[2,8,2,16,16,128]{5,4,3,2,1,0:T(8,128)(2,1)}, bf16[2,8,2,16,16,128]{5,4,3,2,1,0:T(8,128)(2,1)}) custom-call(s32[41]{0:T(128)} %concatenate.19.sc_ref, bf16[64,128,512]{2,1,0:T(8,128)(2,1)} %refs_7_.7, bf16[64,128,512]{2,1,0:T(8,128)(2,1)} %refs_7_.7, bf16[64,128,512]{2,1,0:T(8,128)(2,1)} %refs_7_.7, bf16[64,128,512]{2,1,0:T(8,128)(2,1)} %refs_7_.7, ...), custom_call_target="tpu_custom_call" | custom-call | flops 1207959552 | bytes 16777216 | tf_op jit(solution)/shard_map/degrees/pallas_call | solution.py:239
  182.0 8.6 %collective-permute-done.14 = bf16[8,2,16,16,128]{4,3,2,1,0:T(8,128)(2,1)} collective-permute-done((bf16[8,2,16,16,128]{4,3,2,1,0:T(8,128)(2,1)}, bf16[8,2,16,16,128]{4,3,2,1,0:T(8,128)(2,1)}, u32[]{:S(2)}, u32[]{:S(2)}) %collective-permute-start.14) | collective-permute-done | bytes 1048608 | tf_op jit(solution)/shard_map/ppermute | solution.py:573
  193.6 5.7 %all-to-all-start.5 = ((bf16[8,2,16,16,128]{4,3,2,1,0:T(8,128)(2,1)}), bf16[8,2,16,16,128]{4,3,2,1,0:T(8,128)(2,1)S(1)}, u32[]{:S(2)}, u32[]{:S(2)}) async-start(bf16[8,2,16,16,128]{4,3,2,1,0:T(8,128)(2,1)} %fusion.1), calls=%async_computation.5 | async-start | bytes 2097152 | tf_op jit(solution)/shard_map/all_to_all | solution.py:576
  199.3 13.5 %collective-permute-done.refs_10_ = bf16[8,2,16,16,128]{4,3,2,1,0:T(8,128)(2,1)} collective-permute-done((bf16[8,2,16,16,128]{4,3,2,1,0:T(8,128)(2,1)S(1)}, bf16[8,2,16,16,128]{4,3,2,1,0:T(8,128)(2,1)}, u32[]{:S(2)}, u32[]{:S(2)}) %collective-permute-start) | collective-permute-done | bytes 1048608 | tf_op jit(solution)/shard_map/ppermute | solution.py:573
  217.3 13.8 %degrees.4 = (bf16[2,8,2,16,16,128]{5,4,3,2,1,0:T(8,128)(2,1)}, bf16[2,8,2,16,16,128]{5,4,3,2,1,0:T(8,128)(2,1)}) custom-call(s32[41]{0:T(128)} %concatenate.16.sc_ref, bf16[64,128,512]{2,1,0:T(8,128)(2,1)} %refs_7_.7, bf16[64,128,512]{2,1,0:T(8,128)(2,1)} %refs_7_.7, bf16[64,128,512]{2,1,0:T(8,128)(2,1)} %refs_7_.7, bf16[64,128,512]{2,1,0:T(8,128)(2,1)} %refs_7_.7, ...), custom_call_target="tpu_custom_call" | custom-call | flops 1207959552 | bytes 16777216 | tf_op jit(solution)/shard_map/degrees/pallas_call | solution.py:239
  231.6 9.8 %collective-permute-done.9 = bf16[8,2,16,16,128]{4,3,2,1,0:T(8,128)(2,1)} collective-permute-done((bf16[8,2,16,16,128]{4,3,2,1,0:T(8,128)(2,1)}, bf16[8,2,16,16,128]{4,3,2,1,0:T(8,128)(2,1)}, u32[]{:S(2)}, u32[]{:S(2)}) %collective-permute-start.9) | collective-permute-done | bytes 1048608 | tf_op jit(solution)/shard_map/ppermute | solution.py:573
  244.8 5.7 %all-to-all-start.3 = ((bf16[8,2,16,16,128]{4,3,2,1,0:T(8,128)(2,1)}), bf16[8,2,16,16,128]{4,3,2,1,0:T(8,128)(2,1)S(1)}, u32[]{:S(2)}, u32[]{:S(2)}) async-start(bf16[8,2,16,16,128]{4,3,2,1,0:T(8,128)(2,1)} %fusion.2), calls=%async_computation.3 | async-start | bytes 2097152 | tf_op jit(solution)/shard_map/all_to_all | solution.py:576
  254.0 24.8 %collective-permute-done.19 = bf16[8,2,16,16,128]{4,3,2,1,0:T(8,128)(2,1)S(1)} collective-permute-done((bf16[8,2,16,16,128]{4,3,2,1,0:T(8,128)(2,1)S(1)}, bf16[8,2,16,16,128]{4,3,2,1,0:T(8,128)(2,1)S(1)}, u32[]{:S(2)}, u32[]{:S(2)}) %collective-permute-start.19) | collective-permute-done | bytes 1048608 | tf_op jit(solution)/shard_map/ppermute | solution.py:573
  281.5 5.7 %all-to-all-start.6 = ((bf16[8,2,16,16,128]{4,3,2,1,0:T(8,128)(2,1)}), bf16[8,2,16,16,128]{4,3,2,1,0:T(8,128)(2,1)S(1)}, u32[]{:S(2)}, u32[]{:S(2)}) async-start(bf16[8,2,16,16,128]{4,3,2,1,0:T(8,128)(2,1)} %fusion), calls=%async_computation.6 | async-start | bytes 2097152 | tf_op jit(solution)/shard_map/all_to_all | solution.py:576
  289.3 23.0 %collective-permute-done.4 = bf16[8,2,16,16,128]{4,3,2,1,0:T(8,128)(2,1)S(1)} collective-permute-done((bf16[8,2,16,16,128]{4,3,2,1,0:T(8,128)(2,1)S(1)}, bf16[8,2,16,16,128]{4,3,2,1,0:T(8,128)(2,1)S(1)}, u32[]{:S(2)}, u32[]{:S(2)}) %collective-permute-start.4) | collective-permute-done | bytes 1048608 | tf_op jit(solution)/shard_map/ppermute | solution.py:573
  314.9 5.7 %all-to-all-start.1 = ((bf16[8,2,16,16,128]{4,3,2,1,0:T(8,128)(2,1)}), bf16[8,2,16,16,128]{4,3,2,1,0:T(8,128)(2,1)S(1)}, u32[]{:S(2)}, u32[]{:S(2)}) async-start(bf16[8,2,16,16,128]{4,3,2,1,0:T(8,128)(2,1)} %fusion.3), calls=%async_computation.1 | async-start | bytes 2097152 | tf_op jit(solution)/shard_map/all_to_all | solution.py:576
  320.7 18.9 %synthesis.2.refs_2_ = f32[64,2,16,1024]{3,2,1,0:T(8,128)} custom-call(bf16[256,16,128]{2,1,0:T(8,128)(2,1)} %bitcast.310, bf16[256,16,128]{2,1,0:T(8,128)(2,1)} %bitcast.309, bf16[256,16,128]{2,1,0:T(8,128)(2,1)} %bitcast.311, bf16[256,1024]{1,0:T(8,128)(2,1)} %fusion.87.refs_8_.refs_3_, bf16[256,1024]{1,0:T(8,128)(2,1)} %get-tuple-element.57.refs_8_.refs_4_, ...), custom_call_target="tpu_custom_call" | custom-call | flops 3221225472 | bytes 25165824 | tf_op jit(solution)/shard_map/synthesis/pallas_call | solution.py:419
  343.6 15.8 %synthesis.3 = (f32[2,2,4,1024,128]{4,3,2,1,0:T(8,128)S(1)}, f32[8,128]{1,0:T(8,128)S(1)}, f32[2,2,64,2,8,512]{5,4,3,2,1,0:T(8,128)S(1)}, f32[2,2,64,2,8,512]{5,...) custom-call(bf16[256,16,128]{2,1,0:T(8,128)(2,1)S(1)} %bitcast.278, bf16[256,1024]{1,0:T(8,128)(2,1)S(1)} %copy-done, ...), custom_call_target="tpu_custom_call" | custom-call | flops 1073741824 | bytes 41943040 | tf_op jit(solution)/shard_map/synthesis/pallas_call | solution.py:419
  373.7 9.6 %update.1 = (f32[64,2,16,1024]{3,2,1,0:T(8,128)}, f32[64,2,16,1024]{3,2,1,0:T(8,128)}, f32[64,2,16,1024]{3,2,1,0:T(8,128)}) custom-call(f32[8,128]{1,0:T(8,128)S(1)} %add.884.refs_0_, f32[8,128]{1,0:T(8,128)S(1)} %collective-permute-done.24.refs_1_, f32[8,128]{1,0:T(8,128)S(1)} %collective-permute-done.25.refs_2_, ...), custom_call_target="tpu_custom_call" | custom-call | flops 12582912 | bytes 25165824 | tf_op jit(solution)/shard_map/update/pallas_call | solution.py:480
  (107 shorter events, 76.8 us)
Async XLA Ops:
  13.0 33.1 %all-to-all-start.2 = ((bf16[8,1,32,16,128]{4,3,2,1,0:T(8,128)(2,1)}), bf16[8,1,32,16,128]{4,3,2,1,0:T(8,128)(2,1)S(1)}, u32[]{:S(2)}, u32[]{:S(2)}) async-start(bf16[8,1,32,16,128]{4,3,2,1,0:T(8,128)(2,1)} %analysis.2), calls=%async_computation.2 | async-start | bytes 2097152 | tf_op jit(solution)/shard_map/all_to_all | solution.py:576
  75.8 55.5 %all-to-all-start = ((bf16[8,2,32,16,128]{4,3,2,1,0:T(8,128)(2,1)}), bf16[8,2,32,16,128]{4,3,2,1,0:T(8,128)(2,1)S(1)}, u32[]{:S(2)}, u32[]{:S(2)}) async-start(bf16[8,2,32,16,128]{4,3,2,1,0:T(8,128)(2,1)} %get-tuple-element.24), calls=%async_computation | async-start | bytes 4194304 | tf_op jit(solution)/shard_map/all_to_all | solution.py:576
  79.4 25.3 %collective-permute-start.10 = (bf16[8,2,16,16,128]{4,3,2,1,0:T(8,128)(2,1)}, bf16[8,2,16,16,128]{4,3,2,1,0:T(8,128)(2,1)}, u32[]{:S(2)}, u32[]{:S(2)}) collective-permute-start(bf16[8,2,16,16,128]{4,3,2,1,0:T(8,128)(2,1)} %bitcast.303), channel_id=1, source_target_pairs={{0,2},{1,3},{4,6},{5,7},{8,10},{9,11},{12,14},{13,15},{16,18},{17,... | collective-permute-start | bytes 3145736 | tf_op jit(solution)/shard_map/ppermute | solution.py:573
  83.8 30.6 %collective-permute-start.11 = (bf16[8,2,16,16,128]{4,3,2,1,0:T(8,128)(2,1)}, bf16[8,2,16,16,128]{4,3,2,1,0:T(8,128)(2,1)}, u32[]{:S(2)}, u32[]{:S(2)}) collective-permute-start(bf16[8,2,16,16,128]{4,3,2,1,0:T(8,128)(2,1)} %bitcast.304), channel_id=1, source_target_pairs={{0,1},{1,0},{2,3},{3,2},{4,5},{5,4},{6,7},{7,6},{8,9},{9,8},{10,11... | collective-permute-start | bytes 3145736 | tf_op jit(solution)/shard_map/ppermute | solution.py:601
  104.7 9.7 %collective-permute-start.12 = (bf16[8,2,16,16,128]{4,3,2,1,0:T(8,128)(2,1)}, bf16[8,2,16,16,128]{4,3,2,1,0:T(8,128)(2,1)}, u32[]{:S(2)}, u32[]{:S(2)}) collective-permute-start(bf16[8,2,16,16,128]{4,3,2,1,0:T(8,128)(2,1)} %collective-permute-done.10.refs_10_), channel_id=1, source_target_pairs={{0,1},{1,0},{2,3},{3,2},{4,5},{5,4},{6,7},{7,6},{8,9},{9,8},{10,11... | collective-permute-start | bytes 3145736 | tf_op jit(solution)/shard_map/ppermute | solution.py:601
  104.8 26.5 %collective-permute-start.5 = (bf16[8,2,16,16,128]{4,3,2,1,0:T(8,128)(2,1)S(1)}, bf16[8,2,16,16,128]{4,3,2,1,0:T(8,128)(2,1)}, u32[]{:S(2)}, u32[]{:S(2)}) collective-permute-start(bf16[8,2,16,16,128]{4,3,2,1,0:T(8,128)(2,1)S(1)} %bitcast.300), channel_id=1, source_target_pairs={{0,2},{2,0},{1,3},{3,1},{4,6},{6,4},{5,7},{7,5},{8,10},{10,8},{9,1... | collective-permute-start | bytes 3145736 | tf_op jit(solution)/shard_map/ppermute | solution.py:573
  128.3 31.6 %collective-permute-start.13 = (bf16[2,8,2,16,16,128]{5,4,3,2,1,0:T(8,128)(2,1)}, bf16[2,8,2,16,16,128]{5,4,3,2,1,0:T(8,128)(2,1)}, u32[]{:S(2)}, u32[]{:S(2)}) collective-permute-start(bf16[2,8,2,16,16,128]{5,4,3,2,1,0:T(8,128)(2,1)} %get-tuple-element.32), channel_id=1, source_target_pairs={{0,1},{1,0},{2,3},{3,2},{4,5},{5,4},{6,7},{7,6},{8,9},{9,8},{10,11... | collective-permute-start | bytes 6291464 | tf_op jit(solution)/shard_map/ppermute | solution.py:605
  128.6 9.7 %collective-permute-start.6 = (bf16[8,2,16,16,128]{4,3,2,1,0:T(8,128)(2,1)S(1)}, bf16[8,2,16,16,128]{4,3,2,1,0:T(8,128)(2,1)}, u32[]{:S(2)}, u32[]{:S(2)}) collective-permute-start(bf16[8,2,16,16,128]{4,3,2,1,0:T(8,128)(2,1)S(1)} %bitcast.301), channel_id=1, source_target_pairs={{0,1},{1,0},{2,3},{3,2},{4,5},{5,4},{6,7},{7,6},{8,9},{9,8},{10,11... | collective-permute-start | bytes 3145736 | tf_op jit(solution)/shard_map/ppermute | solution.py:601
  132.9 27.0 %collective-permute-start.15 = (bf16[8,2,16,16,128]{4,3,2,1,0:T(8,128)(2,1)}, bf16[8,2,16,16,128]{4,3,2,1,0:T(8,128)(2,1)}, u32[]{:S(2)}, u32[]{:S(2)}) collective-permute-start(bf16[8,2,16,16,128]{4,3,2,1,0:T(8,128)(2,1)} %bitcast.39.refs_9_), channel_id=1, source_target_pairs={{0,2},{1,3},{4,6},{5,7},{8,10},{9,11},{12,14},{13,15},{16,18},{17,... | collective-permute-start | bytes 3145736 | tf_op jit(solution)/shard_map/ppermute | solution.py:573
  152.2 60.5 %collective-permute-start.8 = (bf16[2,8,2,16,16,128]{5,4,3,2,1,0:T(8,128)(2,1)}, bf16[2,8,2,16,16,128]{5,4,3,2,1,0:T(8,128)(2,1)}, u32[]{:S(2)}, u32[]{:S(2)}) collective-permute-start(bf16[2,8,2,16,16,128]{5,4,3,2,1,0:T(8,128)(2,1)} %get-tuple-element.29), channel_id=1, source_target_pairs={{0,1},{1,0},{2,3},{3,2},{4,5},{5,4},{6,7},{7,6},{8,9},{9,8},{10,11... | collective-permute-start | bytes 6291464 | tf_op jit(solution)/shard_map/ppermute | solution.py:605
  152.5 15.4 %collective-permute-start.16 = (bf16[8,2,16,16,128]{4,3,2,1,0:T(8,128)(2,1)}, bf16[8,2,16,16,128]{4,3,2,1,0:T(8,128)(2,1)}, u32[]{:S(2)}, u32[]{:S(2)}) collective-permute-start(bf16[8,2,16,16,128]{4,3,2,1,0:T(8,128)(2,1)} %bitcast.39.refs_9_), channel_id=1, source_target_pairs={{0,1},{1,0},{2,3},{3,2},{4,5},{5,4},{6,7},{7,6},{8,9},{9,8},{10,11... | collective-permute-start | bytes 3145736 | tf_op jit(solution)/shard_map/ppermute | solution.py:601
  159.9 8.0 %collective-permute-start.17 = (bf16[8,2,16,16,128]{4,3,2,1,0:T(8,128)(2,1)}, bf16[8,2,16,16,128]{4,3,2,1,0:T(8,128)(2,1)}, u32[]{:S(2)}, u32[]{:S(2)}) collective-permute-start(bf16[8,2,16,16,128]{4,3,2,1,0:T(8,128)(2,1)} %collective-permute-done.15.refs_10_), channel_id=1, source_target_pairs={{0,1},{1,0},{2,3},{3,2},{4,5},{5,4},{6,7},{7,6},{8,9},{9,8},{10,11... | collective-permute-start | bytes 3145736 | tf_op jit(solution)/shard_map/ppermute | solution.py:601
  162.4 28.2 %collective-permute-start.14 = (bf16[8,2,16,16,128]{4,3,2,1,0:T(8,128)(2,1)}, bf16[8,2,16,16,128]{4,3,2,1,0:T(8,128)(2,1)}, u32[]{:S(2)}, u32[]{:S(2)}) collective-permute-start(bf16[8,2,16,16,128]{4,3,2,1,0:T(8,128)(2,1)} %fusion.9), channel_id=1, source_target_pairs={{2,0},{3,1},{6,4},{7,5},{10,8},{11,9},{14,12},{15,13},{18,16},{19,... | collective-permute-start | bytes 3145736 | tf_op jit(solution)/shard_map/ppermute | solution.py:573
  163.7 49.1 %collective-permute-start = (bf16[8,2,16,16,128]{4,3,2,1,0:T(8,128)(2,1)S(1)}, bf16[8,2,16,16,128]{4,3,2,1,0:T(8,128)(2,1)}, u32[]{:S(2)}, u32[]{:S(2)}) collective-permute-start(bf16[8,2,16,16,128]{4,3,2,1,0:T(8,128)(2,1)S(1)} %bitcast.307), channel_id=1, source_target_pairs={{0,2},{2,0},{1,3},{3,1},{4,6},{6,4},{5,7},{7,5},{8,10},{10,8},{9,1... | collective-permute-start | bytes 3145736 | tf_op jit(solution)/shard_map/ppermute | solution.py:573
  181.9 68.6 %collective-permute-start.18 = (bf16[2,8,2,16,16,128]{5,4,3,2,1,0:T(8,128)(2,1)}, bf16[2,8,2,16,16,128]{5,4,3,2,1,0:T(8,128)(2,1)}, u32[]{:S(2)}, u32[]{:S(2)}) collective-permute-start(bf16[2,8,2,16,16,128]{5,4,3,2,1,0:T(8,128)(2,1)} %get-tuple-element.34), channel_id=1, source_target_pairs={{0,1},{1,0},{2,3},{3,2},{4,5},{5,4},{6,7},{7,6},{8,9},{9,8},{10,11... | collective-permute-start | bytes 6291464 | tf_op jit(solution)/shard_map/ppermute | solution.py:605
  193.6 51.2 %all-to-all-start.5 = ((bf16[8,2,16,16,128]{4,3,2,1,0:T(8,128)(2,1)}), bf16[8,2,16,16,128]{4,3,2,1,0:T(8,128)(2,1)S(1)}, u32[]{:S(2)}, u32[]{:S(2)}) async-start(bf16[8,2,16,16,128]{4,3,2,1,0:T(8,128)(2,1)} %fusion.1), calls=%async_computation.5 | async-start | bytes 2097152 | tf_op jit(solution)/shard_map/all_to_all | solution.py:576
  199.3 16.9 %collective-permute-start.1 = (bf16[8,2,16,16,128]{4,3,2,1,0:T(8,128)(2,1)S(1)}, bf16[8,2,16,16,128]{4,3,2,1,0:T(8,128)(2,1)S(1)}, u32[]{:S(2)}, u32[]{:S(2)}) collective-permute-start(bf16[8,2,16,16,128]{4,3,2,1,0:T(8,128)(2,1)S(1)} %bitcast.308), channel_id=1, source_target_pairs={{0,1},{1,0},{2,3},{3,2},{4,5},{5,4},{6,7},{7,6},{8,9},{9,8},{10,11... | collective-permute-start | bytes 3145736 | tf_op jit(solution)/shard_map/ppermute | solution.py:601
  215.6 25.9 %collective-permute-start.9 = (bf16[8,2,16,16,128]{4,3,2,1,0:T(8,128)(2,1)}, bf16[8,2,16,16,128]{4,3,2,1,0:T(8,128)(2,1)}, u32[]{:S(2)}, u32[]{:S(2)}) collective-permute-start(bf16[8,2,16,16,128]{4,3,2,1,0:T(8,128)(2,1)} %fusion.7), channel_id=1, source_target_pairs={{0,2},{2,0},{1,3},{3,1},{4,6},{6,4},{5,7},{7,5},{8,10},{10,8},{9,1... | collective-permute-start | bytes 3145736 | tf_op jit(solution)/shard_map/ppermute | solution.py:573
  231.1 56.1 %collective-permute-start.3 = (bf16[2,8,2,16,16,128]{5,4,3,2,1,0:T(8,128)(2,1)}, bf16[2,8,2,16,16,128]{5,4,3,2,1,0:T(8,128)(2,1)}, u32[]{:S(2)}, u32[]{:S(2)}) collective-permute-start(bf16[2,8,2,16,16,128]{5,4,3,2,1,0:T(8,128)(2,1)} %get-tuple-element.26), channel_id=1, source_target_pairs={{0,1},{1,0},{2,3},{3,2},{4,5},{5,4},{6,7},{7,6},{8,9},{9,8},{10,11... | collective-permute-start | bytes 6291464 | tf_op jit(solution)/shard_map/ppermute | solution.py:605
  244.8 36.7 %all-to-all-start.3 = ((bf16[8,2,16,16,128]{4,3,2,1,0:T(8,128)(2,1)}), bf16[8,2,16,16,128]{4,3,2,1,0:T(8,128)(2,1)S(1)}, u32[]{:S(2)}, u32[]{:S(2)}) async-start(bf16[8,2,16,16,128]{4,3,2,1,0:T(8,128)(2,1)} %fusion.2), calls=%async_computation.3 | async-start | bytes 2097152 | tf_op jit(solution)/shard_map/all_to_all | solution.py:576
  252.5 26.3 %collective-permute-start.19 = (bf16[8,2,16,16,128]{4,3,2,1,0:T(8,128)(2,1)S(1)}, bf16[8,2,16,16,128]{4,3,2,1,0:T(8,128)(2,1)S(1)}, u32[]{:S(2)}, u32[]{:S(2)}) collective-permute-start(bf16[8,2,16,16,128]{4,3,2,1,0:T(8,128)(2,1)S(1)} %fusion.11), channel_id=1, source_target_pairs={{2,0},{3,1},{6,4},{7,5},{10,8},{11,9},{14,12},{15,13},{18,16},{19,... | collective-permute-start | bytes 3145736 | tf_op jit(solution)/shard_map/ppermute | solution.py:573
  281.5 33.5 %all-to-all-start.6 = ((bf16[8,2,16,16,128]{4,3,2,1,0:T(8,128)(2,1)}), bf16[8,2,16,16,128]{4,3,2,1,0:T(8,128)(2,1)S(1)}, u32[]{:S(2)}, u32[]{:S(2)}) async-start(bf16[8,2,16,16,128]{4,3,2,1,0:T(8,128)(2,1)} %fusion), calls=%async_computation.6 | async-start | bytes 2097152 | tf_op jit(solution)/shard_map/all_to_all | solution.py:576
  289.2 23.1 %collective-permute-start.4 = (bf16[8,2,16,16,128]{4,3,2,1,0:T(8,128)(2,1)S(1)}, bf16[8,2,16,16,128]{4,3,2,1,0:T(8,128)(2,1)S(1)}, u32[]{:S(2)}, u32[]{:S(2)}) collective-permute-start(bf16[8,2,16,16,128]{4,3,2,1,0:T(8,128)(2,1)S(1)} %fusion.5), channel_id=1, source_target_pairs={{0,2},{2,0},{1,3},{3,1},{4,6},{6,4},{5,7},{7,5},{8,10},{10,8},{9,1... | collective-permute-start | bytes 3145736 | tf_op jit(solution)/shard_map/ppermute | solution.py:573
  314.9 28.7 %all-to-all-start.1 = ((bf16[8,2,16,16,128]{4,3,2,1,0:T(8,128)(2,1)}), bf16[8,2,16,16,128]{4,3,2,1,0:T(8,128)(2,1)S(1)}, u32[]{:S(2)}, u32[]{:S(2)}) async-start(bf16[8,2,16,16,128]{4,3,2,1,0:T(8,128)(2,1)} %fusion.3), calls=%async_computation.1 | async-start | bytes 2097152 | tf_op jit(solution)/shard_map/all_to_all | solution.py:576
  (19 other events, 250.1 us)

commit v3 on v2

--- a/solution.py
+++ b/solution.py
@@ -137,7 +137,7 @@
     )(*[direction4] * parts_n, *tables)
 
 
-def degree_call(scalars, legendre, temporal, gathered, n_x):
+def degree_call(scalars, legendre, temporal, gathered):
     _, deg_dev, lat_all = legendre.shape
     time_all = temporal.shape[-1]
     n_pieces = len(gathered)
@@ -155,7 +155,8 @@
     def kernel(sc_ref, *refs):
         leg_refs, tmp_ref, refs = refs[:kb], refs[kb], refs[kb + 1 :]
         r_refs = refs[:n_pieces]
-        keep_ref, send_ref, c_ref, r_scr, g_scr = refs[n_pieces:]
+        out_refs = refs[n_pieces : 2 * n_pieces]
+        c_ref, r_scr, g_scr = refs[2 * n_pieces :]
         step = pl.program_id(0)
         low = low_half((hi_n, LANES))
 
@@ -212,15 +213,15 @@
                     ).astype(BF)
                 for q in range(n_pieces):
                     base = sc_ref[1 + n_pieces + q] * time_dev
-                    out = keep_ref if q < n_x else send_ref
+                    out = out_refs[q]
                     for c in range(2):
                         for p in range(nb // 2):
                             at = pl.multiple_of(c * time_all + base, hi_n)
                             lanes = slice(p * LANES, (p + 1) * LANES)
                             v0 = g_scr[kk, pl.ds(at, hi_n), lanes]
                             v1 = g_scr[kk, pl.ds(at + hi_n, hi_n), lanes]
-                            out[q % n_x, 2 * p, c, kk] = jnp.where(low, v0, swap_halves(v1))
-                            out[q % n_x, 2 * p + 1, c, kk] = jnp.where(low, swap_halves(v0), v1)
+                            out[2 * p, c, kk] = jnp.where(low, v0, swap_halves(v1))
+                            out[2 * p + 1, c, kk] = jnp.where(low, swap_halves(v0), v1)
 
     def leg_spec(kk):
         def index(s, sc):
@@ -231,14 +232,14 @@
 
     piece = (nb, 2, chunk_n, hi_n, LANES)
     out_block = pl.BlockSpec(
-        (n_x, nb, 2, kb, hi_n, LANES),
-        lambda s, sc: (0, 0, 0, jnp.maximum(s - n1 - n2, 0), 0, 0),
+        (nb, 2, kb, hi_n, LANES),
+        lambda s, sc: (0, 0, jnp.maximum(s - n1 - n2, 0), 0, 0),
     )
-    out_shape = jax.ShapeDtypeStruct((n_x,) + piece, BF)
+    out_shape = jax.ShapeDtypeStruct(piece, BF)
     flops = 4 * chunk_n * deg_dev * lat_all * rows + 2 * deg_dev * 2 * chunk_n * time_all**2
     return pl.pallas_call(
         kernel,
-        out_shape=(out_shape, out_shape),
+        out_shape=(out_shape,) * n_pieces,
         grid_spec=pltpu.PrefetchScalarGridSpec(
             num_scalar_prefetch=1,
             grid=(n1 + n2 + n1,),
@@ -256,7 +257,7 @@
                 )
             ]
             * n_pieces,
-            out_specs=(out_block, out_block),
+            out_specs=(out_block,) * n_pieces,
             scratch_shapes=[
                 pltpu.VMEM((2 * chunk_n * pitch, time_all), F32),
                 pltpu.VMEM((kb, rows, lat_all), BF),
@@ -601,12 +602,15 @@
         pieces = own + [lax.ppermute(v, "core", swap) for v in own]
         span = slice(start * chunk_n, (start + 1) * chunk_n)
         scalars = jnp.concatenate([header, own_orders[high, span], own_rows[high, span]])
-        keep, send = degree_call(scalars, legendre, temporal_narrow, pieces, n_x)
-        other = lax.ppermute(send, "core", swap)
-        halves = [keep[s].astype(F32) + other[s].astype(F32) for s in range(n_x)]
-        halves = [halves[0].astype(BF)] + [v.astype(BF) for v in halves[1:]]
-        parts = [shift(halves[s], s, backward) for s in range(1, n_x)]
-        total = halves[0].astype(F32)
+        out = degree_call(scalars, legendre, temporal_narrow, pieces)
+        keep, send = out[:n_x], out[n_x:]
+        other = [lax.ppermute(send[s], "core", swap) for s in range(1, n_x)]
+        halves = [
+            (keep[s].astype(F32) + other[s - 1].astype(F32)).astype(BF) for s in range(1, n_x)
+        ]
+        parts = [shift(halves[s - 1], s, backward) for s in range(1, n_x)]
+        near = lax.ppermute(send[0], "core", swap)
+        total = keep[0].astype(F32) + near.astype(F32)
         for part in parts:
             total = total + part.astype(F32)
         total = total.astype(BF)

time: 384 us -> 377 us (0.982)
  waiting for transfers between devices: 132 us -> 127 us
    ppermute x8, waiting for transfers between devices: 110 us -> 99.9 us  [shift(): return lax.ppermute(v, 'x', [pair for pair in pairs if keep(*pair)])]
  transfers between devices with their start and end apart: 33 -> 37, of which waited for: 16 -> 17; matrix products, arithmetic and copies ran while one was open for 9% -> 9% of each run, Pallas kernels for 23% -> 24%
where the time goes in v3:
time: 377 us; the launch traced here: 376 us
  waiting for transfers between devices  127 us (34%)
  Pallas kernels  124 us (33%)
  starting transfers between devices  57.5 us (15%)
  other arithmetic  29.9 us (8%)
  blocking collectives  29.7 us (8%)
  local copies, waits for them, and re-layouts  6.46 us (2%)
    ppermute x8, waiting for transfers between devices, shift(): return lax.ppermute(v, 'x', [pair for pair in pairs if keep(*pair)])  99.9 us
    pallas_call x4, Pallas kernels, degree_call(): pl.pallas_call(kernel, out_shape=(out_shape,) * n_pieces, grid_spec=pltpu...  56 us
    pallas_call x2, Pallas kernels, synthesis_call(): pl.pallas_call(kernel, out_shape=tuple(out_shape), grid=(hi_n // sub, len...  34.7 us
    all_to_all x6, starting transfers between devices, across(): return lax.all_to_all(v, 'blk', split_axis=0, concat_axis=0, tiled=True)  34.5 us
    all_to_all x1, blocking collectives, across(): return lax.all_to_all(v, 'blk', split_axis=0, concat_axis=0, tiled=True)  29.7 us
    pallas_call x2, Pallas kernels, analysis_call(): pl.pallas_call(kernel, out_shape=tuple((jax.ShapeDtypeStruct(shape, BF) f...  23.9 us
    ppermute x8, starting transfers between devices, shift(): return lax.ppermute(v, 'x', [pair for pair in pairs if keep(*pair)])  15.7 us
    all_to_all x6, waiting for transfers between devices, across(): return lax.all_to_all(v, 'blk', split_axis=0, concat_axis=0, tiled=True)  14.6 us
  transfers between devices with their start and end apart: 37, of which 17 were waited for; matrix products, arithmetic and copies ran while one was open for 9% of the time, Pallas kernels for 24%

profile of v3, /device:TPU:0, one launch (start us, length us, event | category | flops | bytes accessed | tf_op | source)
XLA Modules:
  0.0 375.7 jit_solution(4898524052911266069)
XLA Ops:
  3.4 9.7 %analysis.2 = bf16[8,1,32,16,128]{4,3,2,1,0:T(8,128)(2,1)} custom-call(f32[64,2,16,1024]{3,2,1,0:T(8,128)} %bitcast.251, f32[64,2,16,1024]{3,2,1,0:T(8,128)} %bitcast.252, f32[64,2,16,1024]{3,2,1,0:T(8,128)} %bitcast.253, f32[64,2,16,1024]{3,2,1,0:T(8,128)} %bitcast.254, f32[64,2,16,1024]{3,2,1,0:T(8,128)} %bitcast.255, f32[64,2,16,1024]{3,2,1,0:T(8,128)} %bitcast.256, ...), custom_call_target="tpu_custom_call" | custom-call | flops 1073741824 | bytes 8912896 | tf_op jit(solution)/shard_map/analysis/pallas_call | solution.py:119
  13.0 7.3 %all-to-all-start.2 = ((bf16[8,1,32,16,128]{4,3,2,1,0:T(8,128)(2,1)}), bf16[8,1,32,16,128]{4,3,2,1,0:T(8,128)(2,1)S(1)}, u32[]{:S(2)}, u32[]{:S(2)}) async-start(bf16[8,1,32,16,128]{4,3,2,1,0:T(8,128)(2,1)} %analysis.2), calls=%async_computation.2 | async-start | bytes 2097152 | tf_op jit(solution)/shard_map/all_to_all | solution.py:577
  24.0 14.2 %analysis.3 = (bf16[8,1,32,16,128]{4,3,2,1,0:T(8,128)(2,1)}, bf16[8,2,32,16,128]{4,3,2,1,0:T(8,128)(2,1)}) custom-call(f32[64,2,16,1024]{3,2,1,0:T(8,128)} %bitcast.259, f32[64,2,16,1024]{3,2,1,0:T(8,128)} %bitcast.260, f32[64,2,16,1024]{3,2,1,0:T(8,128)} %bitcast.261, f32[64,2,16,1024]{3,2,1,0:T(8,128)} %bitcast.262, f32[64,2,16,1024]{3,2,1,0:T(8,128)} %bitcast.263, ...), custom_call_target="tpu_custom_call" | custom-call | flops 3221225472 | bytes 9961472 | tf_op jit(solution)/shard_map/analysis/pallas_call | solution.py:119
  38.3 7.8 %all-to-all-done.2 = bf16[8,1,32,16,128]{4,3,2,1,0:T(8,128)(2,1)S(1)} async-done(((bf16[8,1,32,16,128]{4,3,2,1,0:T(8,128)(2,1)}), bf16[8,1,32,16,128]{4,3,2,1,0:T(8,128)(2,1)S(1)}, u32[]{:S(2)}, u32[]{:S(2)}) %all-to-all-start.2) | async-done | bytes 1048608 | tf_op jit(solution)/shard_map/all_to_all | solution.py:577
  46.1 29.7 %all_to_all.35 = bf16[8,1,32,16,128]{4,3,2,1,0:T(8,128)(2,1)} all-to-all(bf16[8,1,32,16,128]{4,3,2,1,0:T(8,128)(2,1)} %get-tuple-element.42), channel_id=1, replica_groups=mesh['blk'=8,'x'=2,'core'=2] {'blk'}, dimensions={0} | all-to-all | bytes 2097152 | tf_op jit(solution)/shard_map/all_to_all | solution.py:577
  83.8 20.9 %collective-permute-done.12.refs_10_ = bf16[8,2,16,16,128]{4,3,2,1,0:T(8,128)(2,1)} collective-permute-done((bf16[8,2,16,16,128]{4,3,2,1,0:T(8,128)(2,1)}, bf16[8,2,16,16,128]{4,3,2,1,0:T(8,128)(2,1)}, u32[]{:S(2)}, u32[]{:S(2)}) %collective-permute-start.12) | collective-permute-done | bytes 1048608 | tf_op jit(solution)/shard_map/ppermute | solution.py:574
  104.7 6.4 %convert_element_type.119.refs_8_ = bf16[128,128,128]{2,1,0:T(8,128)(2,1)} convert(f32[128,128,128]{2,1,0:T(8,128)} %param.12) | non-fusion elementwise | flops 2097152 | bytes 12582912 | tf_op jit(solution)/shard_map/convert_element_type | solution.py:586
  114.4 13.9 %degrees.6 = (bf16[8,2,16,16,128]{4,3,2,1,0:T(8,128)(2,1)}, bf16[8,2,16,16,128]{4,3,2,1,0:T(8,128)(2,1)}, bf16[8,2,16,16,128]{4,3,2,1,0:T(8,128)(2,1)}, bf16[8,2,16,16,128]{4,3,2,1,0:T(8,128)(2,1)}) custom-call(s32[41]{0:T(128)} %concatenate.18.sc_ref, bf16[64,128,512]{2,1,0:T(8,128)(2,1)} %refs_7_.7, bf16[64,128,512]{2,1,0:T(8,128)(2,1)} %refs_7_.7, ...), custom_call_target="tpu_custom_call" | custom-call | flops 1207959552 | bytes 16777216 | tf_op jit(solution)/shard_map/degrees/pallas_call | solution.py:240
  128.9 8.7 %collective-permute-done.6.refs_10_ = bf16[8,2,16,16,128]{4,3,2,1,0:T(8,128)(2,1)} collective-permute-done((bf16[8,2,16,16,128]{4,3,2,1,0:T(8,128)(2,1)S(1)}, bf16[8,2,16,16,128]{4,3,2,1,0:T(8,128)(2,1)}, u32[]{:S(2)}, u32[]{:S(2)}) %collective-permute-start.6) | collective-permute-done | bytes 1048608 | tf_op jit(solution)/shard_map/ppermute | solution.py:574
  147.0 14.1 %degrees.5 = (bf16[8,2,16,16,128]{4,3,2,1,0:T(8,128)(2,1)}, bf16[8,2,16,16,128]{4,3,2,1,0:T(8,128)(2,1)}, bf16[8,2,16,16,128]{4,3,2,1,0:T(8,128)(2,1)}, bf16[8,2,16,16,128]{4,3,2,1,0:T(8,128)(2,1)}) custom-call(s32[41]{0:T(128)} %concatenate.17.sc_ref, bf16[64,128,512]{2,1,0:T(8,128)(2,1)} %refs_7_.7, bf16[64,128,512]{2,1,0:T(8,128)(2,1)} %refs_7_.7, ...), custom_call_target="tpu_custom_call" | custom-call | flops 1207959552 | bytes 16777216 | tf_op jit(solution)/shard_map/degrees/pallas_call | solution.py:240
  166.4 5.8 %collective-permute-done.17 = bf16[8,2,16,16,128]{4,3,2,1,0:T(8,128)(2,1)} collective-permute-done((bf16[8,2,16,16,128]{4,3,2,1,0:T(8,128)(2,1)S(1)}, bf16[8,2,16,16,128]{4,3,2,1,0:T(8,128)(2,1)}, u32[]{:S(2)}, u32[]{:S(2)}) %collective-permute-start.17) | collective-permute-done | bytes 1048608 | tf_op jit(solution)/shard_map/ppermute | solution.py:574
  175.2 5.8 %all-to-all-start.5 = ((bf16[8,2,16,16,128]{4,3,2,1,0:T(8,128)(2,1)}), bf16[8,2,16,16,128]{4,3,2,1,0:T(8,128)(2,1)S(1)}, u32[]{:S(2)}, u32[]{:S(2)}) async-start(bf16[8,2,16,16,128]{4,3,2,1,0:T(8,128)(2,1)} %add_convert_fusion.2), calls=%async_computation.5 | async-start | bytes 2097152 | tf_op jit(solution)/shard_map/all_to_all | solution.py:577
  186.7 14.0 %degrees.7 = (bf16[8,2,16,16,128]{4,3,2,1,0:T(8,128)(2,1)}, bf16[8,2,16,16,128]{4,3,2,1,0:T(8,128)(2,1)}, bf16[8,2,16,16,128]{4,3,2,1,0:T(8,128)(2,1)}, bf16[8,2,16,16,128]{4,3,2,1,0:T(8,128)(2,1)}) custom-call(s32[41]{0:T(128)} %concatenate.19.sc_ref, bf16[64,128,512]{2,1,0:T(8,128)(2,1)} %refs_7_.7, bf16[64,128,512]{2,1,0:T(8,128)(2,1)} %refs_7_.7, ...), custom_call_target="tpu_custom_call" | custom-call | flops 1207959552 | bytes 16777216 | tf_op jit(solution)/shard_map/degrees/pallas_call | solution.py:240
  201.2 6.1 %collective-permute-done.refs_10_ = bf16[8,2,16,16,128]{4,3,2,1,0:T(8,128)(2,1)} collective-permute-done((bf16[8,2,16,16,128]{4,3,2,1,0:T(8,128)(2,1)S(1)}, bf16[8,2,16,16,128]{4,3,2,1,0:T(8,128)(2,1)}, u32[]{:S(2)}, u32[]{:S(2)}) %collective-permute-start) | collective-permute-done | bytes 1048608 | tf_op jit(solution)/shard_map/ppermute | solution.py:574
  207.3 20.6 %collective-permute-done.11 = bf16[8,2,16,16,128]{4,3,2,1,0:T(8,128)(2,1)} collective-permute-done((bf16[8,2,16,16,128]{4,3,2,1,0:T(8,128)(2,1)}, bf16[8,2,16,16,128]{4,3,2,1,0:T(8,128)(2,1)}, u32[]{:S(2)}, u32[]{:S(2)}) %collective-permute-start.11) | collective-permute-done | bytes 1048608 | tf_op jit(solution)/shard_map/ppermute | solution.py:574
  242.9 14.0 %degrees.4 = (bf16[8,2,16,16,128]{4,3,2,1,0:T(8,128)(2,1)}, bf16[8,2,16,16,128]{4,3,2,1,0:T(8,128)(2,1)}, bf16[8,2,16,16,128]{4,3,2,1,0:T(8,128)(2,1)}, bf16[8,2,16,16,128]{4,3,2,1,0:T(8,128)(2,1)}) custom-call(s32[41]{0:T(128)} %concatenate.16.sc_ref, bf16[64,128,512]{2,1,0:T(8,128)(2,1)} %refs_7_.7, bf16[64,128,512]{2,1,0:T(8,128)(2,1)} %refs_7_.7, ...), custom_call_target="tpu_custom_call" | custom-call | flops 1207959552 | bytes 16777216 | tf_op jit(solution)/shard_map/degrees/pallas_call | solution.py:240
  257.4 10.0 %collective-permute-done.23 = bf16[8,2,16,16,128]{4,3,2,1,0:T(8,128)(2,1)} collective-permute-done((bf16[8,2,16,16,128]{4,3,2,1,0:T(8,128)(2,1)}, bf16[8,2,16,16,128]{4,3,2,1,0:T(8,128)(2,1)}, u32[]{:S(2)}, u32[]{:S(2)}) %collective-permute-start.23) | collective-permute-done | bytes 1048608 | tf_op jit(solution)/shard_map/ppermute | solution.py:574
  270.4 6.1 %all-to-all-start.6 = ((bf16[8,2,16,16,128]{4,3,2,1,0:T(8,128)(2,1)}), bf16[8,2,16,16,128]{4,3,2,1,0:T(8,128)(2,1)S(1)}, u32[]{:S(2)}, u32[]{:S(2)}) async-start(bf16[8,2,16,16,128]{4,3,2,1,0:T(8,128)(2,1)} %add_convert_fusion), calls=%async_computation.6 | async-start | bytes 2097152 | tf_op jit(solution)/shard_map/all_to_all | solution.py:577
  279.5 23.1 %collective-permute-done.5 = bf16[8,2,16,16,128]{4,3,2,1,0:T(8,128)(2,1)S(1)} collective-permute-done((bf16[8,2,16,16,128]{4,3,2,1,0:T(8,128)(2,1)S(1)}, bf16[8,2,16,16,128]{4,3,2,1,0:T(8,128)(2,1)S(1)}, u32[]{:S(2)}, u32[]{:S(2)}) %collective-permute-start.5) | collective-permute-done | bytes 1048608 | tf_op jit(solution)/shard_map/ppermute | solution.py:574
  304.0 5.9 %all-to-all-start.1 = ((bf16[8,2,16,16,128]{4,3,2,1,0:T(8,128)(2,1)}), bf16[8,2,16,16,128]{4,3,2,1,0:T(8,128)(2,1)S(1)}, u32[]{:S(2)}, u32[]{:S(2)}) async-start(bf16[8,2,16,16,128]{4,3,2,1,0:T(8,128)(2,1)} %add_convert_fusion.6), calls=%async_computation.1 | async-start | bytes 2097152 | tf_op jit(solution)/shard_map/all_to_all | solution.py:577
  310.0 18.9 %synthesis.2.refs_2_ = f32[64,2,16,1024]{3,2,1,0:T(8,128)} custom-call(bf16[256,16,128]{2,1,0:T(8,128)(2,1)} %bitcast.25.refs_0_, bf16[256,16,128]{2,1,0:T(8,128)(2,1)} %bitcast.281, bf16[256,16,128]{2,1,0:T(8,128)(2,1)} %bitcast.282, bf16[256,1024]{1,0:T(8,128)(2,1)} %fusion.75.refs_8_.refs_3_, bf16[256,1024]{1,0:T(8,128)(2,1)} %get-tuple-element.73.refs_8_.refs_4_, ...), custom_call_target="tpu_custom_call" | custom-call | flops 3221225472 | bytes 25165824 | tf_op jit(solution)/shard_map/synthesis/pallas_call | solution.py:420
  328.8 6.8 %all-to-all-done.1 = bf16[8,2,16,16,128]{4,3,2,1,0:T(8,128)(2,1)S(1)} async-done(((bf16[8,2,16,16,128]{4,3,2,1,0:T(8,128)(2,1)}), bf16[8,2,16,16,128]{4,3,2,1,0:T(8,128)(2,1)S(1)}, u32[]{:S(2)}, u32[]{:S(2)}) %all-to-all-start.1) | async-done | bytes 1048608 | tf_op jit(solution)/shard_map/all_to_all | solution.py:577
  335.6 15.8 %synthesis.3 = (f32[2,2,4,1024,128]{4,3,2,1,0:T(8,128)S(1)}, f32[8,128]{1,0:T(8,128)S(1)}, f32[2,2,64,2,8,512]{5,4,3,2,1,0:T(8,128)S(1)}, f32[2,2,64,2,8,512]{5,...) custom-call(bf16[256,16,128]{2,1,0:T(8,128)(2,1)S(1)} %bitcast.250, bf16[256,1024]{1,0:T(8,128)(2,1)S(1)} %copy-done, ...), custom_call_target="tpu_custom_call" | custom-call | flops 1073741824 | bytes 41943040 | tf_op jit(solution)/shard_map/synthesis/pallas_call | solution.py:420
  366.1 9.6 %update.1 = (f32[64,2,16,1024]{3,2,1,0:T(8,128)}, f32[64,2,16,1024]{3,2,1,0:T(8,128)}, f32[64,2,16,1024]{3,2,1,0:T(8,128)}) custom-call(f32[8,128]{1,0:T(8,128)S(1)} %add.844.refs_0_, f32[8,128]{1,0:T(8,128)S(1)} %collective-permute-done.28.refs_1_, f32[8,128]{1,0:T(8,128)S(1)} %collective-permute-done.29.refs_2_, ...), custom_call_target="tpu_custom_call" | custom-call | flops 12582912 | bytes 25165824 | tf_op jit(solution)/shard_map/update/pallas_call | solution.py:481
  (119 shorter events, 79.5 us)
Async XLA Ops:
  13.0 33.1 %all-to-all-start.2 = ((bf16[8,1,32,16,128]{4,3,2,1,0:T(8,128)(2,1)}), bf16[8,1,32,16,128]{4,3,2,1,0:T(8,128)(2,1)S(1)}, u32[]{:S(2)}, u32[]{:S(2)}) async-start(bf16[8,1,32,16,128]{4,3,2,1,0:T(8,128)(2,1)} %analysis.2), calls=%async_computation.2 | async-start | bytes 2097152 | tf_op jit(solution)/shard_map/all_to_all | solution.py:577
  75.8 61.9 %all-to-all-start = ((bf16[8,2,32,16,128]{4,3,2,1,0:T(8,128)(2,1)}), bf16[8,2,32,16,128]{4,3,2,1,0:T(8,128)(2,1)S(1)}, u32[]{:S(2)}, u32[]{:S(2)}) async-start(bf16[8,2,32,16,128]{4,3,2,1,0:T(8,128)(2,1)} %get-tuple-element.32), calls=%async_computation | async-start | bytes 4194304 | tf_op jit(solution)/shard_map/all_to_all | solution.py:577
  79.4 25.3 %collective-permute-start.12 = (bf16[8,2,16,16,128]{4,3,2,1,0:T(8,128)(2,1)}, bf16[8,2,16,16,128]{4,3,2,1,0:T(8,128)(2,1)}, u32[]{:S(2)}, u32[]{:S(2)}) collective-permute-start(bf16[8,2,16,16,128]{4,3,2,1,0:T(8,128)(2,1)} %bitcast.275), channel_id=1, source_target_pairs={{0,2},{1,3},{4,6},{5,7},{8,10},{9,11},{12,14},{13,15},{16,18},{17,... | collective-permute-start | bytes 3145736 | tf_op jit(solution)/shard_map/ppermute | solution.py:574
  83.8 30.6 %collective-permute-start.13 = (bf16[8,2,16,16,128]{4,3,2,1,0:T(8,128)(2,1)}, bf16[8,2,16,16,128]{4,3,2,1,0:T(8,128)(2,1)}, u32[]{:S(2)}, u32[]{:S(2)}) collective-permute-start(bf16[8,2,16,16,128]{4,3,2,1,0:T(8,128)(2,1)} %bitcast.276), channel_id=1, source_target_pairs={{0,1},{1,0},{2,3},{3,2},{4,5},{5,4},{6,7},{7,6},{8,9},{9,8},{10,11... | collective-permute-start | bytes 3145736 | tf_op jit(solution)/shard_map/ppermute | solution.py:602
  111.2 26.5 %collective-permute-start.6 = (bf16[8,2,16,16,128]{4,3,2,1,0:T(8,128)(2,1)S(1)}, bf16[8,2,16,16,128]{4,3,2,1,0:T(8,128)(2,1)}, u32[]{:S(2)}, u32[]{:S(2)}) collective-permute-start(bf16[8,2,16,16,128]{4,3,2,1,0:T(8,128)(2,1)S(1)} %bitcast.272), channel_id=1, source_target_pairs={{0,2},{2,0},{1,3},{3,1},{4,6},{6,4},{5,7},{7,5},{8,10},{10,8},{9,1... | collective-permute-start | bytes 3145736 | tf_op jit(solution)/shard_map/ppermute | solution.py:574
  139.3 27.0 %collective-permute-start.18 = (bf16[8,2,16,16,128]{4,3,2,1,0:T(8,128)(2,1)}, bf16[8,2,16,16,128]{4,3,2,1,0:T(8,128)(2,1)S(1)}, u32[]{:S(2)}, u32[]{:S(2)}) collective-permute-start(bf16[8,2,16,16,128]{4,3,2,1,0:T(8,128)(2,1)} %bitcast.33.refs_9_), channel_id=1, source_target_pairs={{0,2},{1,3},{4,6},{5,7},{8,10},{9,11},{12,14},{13,15},{16,18},{17,... | collective-permute-start | bytes 3145736 | tf_op jit(solution)/shard_map/ppermute | solution.py:574
  143.0 23.3 %collective-permute-start.15 = (bf16[8,2,16,16,128]{4,3,2,1,0:T(8,128)(2,1)}, bf16[8,2,16,16,128]{4,3,2,1,0:T(8,128)(2,1)}, u32[]{:S(2)}, u32[]{:S(2)}) collective-permute-start(bf16[8,2,16,16,128]{4,3,2,1,0:T(8,128)(2,1)} %get-tuple-element.44), channel_id=1, source_target_pairs={{0,1},{1,0},{2,3},{3,2},{4,5},{5,4},{6,7},{7,6},{8,9},{9,8},{10,11... | collective-permute-start | bytes 3145736 | tf_op jit(solution)/shard_map/ppermute | solution.py:612
  144.8 27.4 %collective-permute-start.17 = (bf16[8,2,16,16,128]{4,3,2,1,0:T(8,128)(2,1)S(1)}, bf16[8,2,16,16,128]{4,3,2,1,0:T(8,128)(2,1)}, u32[]{:S(2)}, u32[]{:S(2)}) collective-permute-start(bf16[8,2,16,16,128]{4,3,2,1,0:T(8,128)(2,1)S(1)} %add_convert_fusion.3), channel_id=1, source_target_pairs={{2,0},{3,1},{6,4},{7,5},{10,8},{11,9},{14,12},{15,13},{18,16},{19,... | collective-permute-start | bytes 3145736 | tf_op jit(solution)/shard_map/ppermute | solution.py:574
  161.1 20.1 %collective-permute-start.10 = (bf16[8,2,16,16,128]{4,3,2,1,0:T(8,128)(2,1)}, bf16[8,2,16,16,128]{4,3,2,1,0:T(8,128)(2,1)}, u32[]{:S(2)}, u32[]{:S(2)}) collective-permute-start(bf16[8,2,16,16,128]{4,3,2,1,0:T(8,128)(2,1)} %get-tuple-element.41), channel_id=1, source_target_pairs={{0,1},{1,0},{2,3},{3,2},{4,5},{5,4},{6,7},{7,6},{8,9},{9,8},{10,11... | collective-permute-start | bytes 3145736 | tf_op jit(solution)/shard_map/ppermute | solution.py:607
  161.5 25.2 %collective-permute-start.19 = (bf16[8,2,16,16,128]{4,3,2,1,0:T(8,128)(2,1)}, bf16[8,2,16,16,128]{4,3,2,1,0:T(8,128)(2,1)}, u32[]{:S(2)}, u32[]{:S(2)}) collective-permute-start(bf16[8,2,16,16,128]{4,3,2,1,0:T(8,128)(2,1)} %bitcast.33.refs_9_), channel_id=1, source_target_pairs={{0,1},{1,0},{2,3},{3,2},{4,5},{5,4},{6,7},{7,6},{8,9},{9,8},{10,11... | collective-permute-start | bytes 3145736 | tf_op jit(solution)/shard_map/ppermute | solution.py:602
  166.4 20.4 %collective-permute-start.20 = (bf16[8,2,16,16,128]{4,3,2,1,0:T(8,128)(2,1)S(1)}, bf16[8,2,16,16,128]{4,3,2,1,0:T(8,128)(2,1)}, u32[]{:S(2)}, u32[]{:S(2)}) collective-permute-start(bf16[8,2,16,16,128]{4,3,2,1,0:T(8,128)(2,1)S(1)} %collective-permute-done.18.refs_10_), channel_id=1, source_target_pairs={{0,1},{1,0},{2,3},{3,2},{4,5},{5,4},{6,7},{7,6},{8,9},{9,8},{10,11... | collective-permute-start | bytes 3145736 | tf_op jit(solution)/shard_map/ppermute | solution.py:602
  175.2 56.0 %all-to-all-start.5 = ((bf16[8,2,16,16,128]{4,3,2,1,0:T(8,128)(2,1)}), bf16[8,2,16,16,128]{4,3,2,1,0:T(8,128)(2,1)S(1)}, u32[]{:S(2)}, u32[]{:S(2)}) async-start(bf16[8,2,16,16,128]{4,3,2,1,0:T(8,128)(2,1)} %add_convert_fusion.2), calls=%async_computation.5 | async-start | bytes 2097152 | tf_op jit(solution)/shard_map/all_to_all | solution.py:577
  181.1 26.2 %collective-permute-start = (bf16[8,2,16,16,128]{4,3,2,1,0:T(8,128)(2,1)S(1)}, bf16[8,2,16,16,128]{4,3,2,1,0:T(8,128)(2,1)}, u32[]{:S(2)}, u32[]{:S(2)}) collective-permute-start(bf16[8,2,16,16,128]{4,3,2,1,0:T(8,128)(2,1)S(1)} %bitcast.279), channel_id=1, source_target_pairs={{0,2},{2,0},{1,3},{3,1},{4,6},{6,4},{5,7},{7,5},{8,10},{10,8},{9,1... | collective-permute-start | bytes 3145736 | tf_op jit(solution)/shard_map/ppermute | solution.py:574
  181.2 26.1 %collective-permute-start.9 = (bf16[8,2,16,16,128]{4,3,2,1,0:T(8,128)(2,1)}, bf16[8,2,16,16,128]{4,3,2,1,0:T(8,128)(2,1)}, u32[]{:S(2)}, u32[]{:S(2)}) collective-permute-start(bf16[8,2,16,16,128]{4,3,2,1,0:T(8,128)(2,1)} %get-tuple-element.39), channel_id=1, source_target_pairs={{0,1},{1,0},{2,3},{3,2},{4,5},{5,4},{6,7},{7,6},{8,9},{9,8},{10,11... | collective-permute-start | bytes 3145736 | tf_op jit(solution)/shard_map/ppermute | solution.py:612
  184.1 43.8 %collective-permute-start.11 = (bf16[8,2,16,16,128]{4,3,2,1,0:T(8,128)(2,1)}, bf16[8,2,16,16,128]{4,3,2,1,0:T(8,128)(2,1)}, u32[]{:S(2)}, u32[]{:S(2)}) collective-permute-start(bf16[8,2,16,16,128]{4,3,2,1,0:T(8,128)(2,1)} %add_convert_fusion.5), channel_id=1, source_target_pairs={{0,2},{2,0},{1,3},{3,1},{4,6},{6,4},{5,7},{7,5},{8,10},{10,8},{9,1... | collective-permute-start | bytes 3145736 | tf_op jit(solution)/shard_map/ppermute | solution.py:574
  200.7 36.3 %collective-permute-start.22 = (bf16[8,2,16,16,128]{4,3,2,1,0:T(8,128)(2,1)}, bf16[8,2,16,16,128]{4,3,2,1,0:T(8,128)(2,1)}, u32[]{:S(2)}, u32[]{:S(2)}) collective-permute-start(bf16[8,2,16,16,128]{4,3,2,1,0:T(8,128)(2,1)} %get-tuple-element.50), channel_id=1, source_target_pairs={{0,1},{1,0},{2,3},{3,2},{4,5},{5,4},{6,7},{7,6},{8,9},{9,8},{10,11... | collective-permute-start | bytes 3145736 | tf_op jit(solution)/shard_map/ppermute | solution.py:607
  201.0 40.9 %collective-permute-start.1 = (bf16[8,2,16,16,128]{4,3,2,1,0:T(8,128)(2,1)S(1)}, bf16[8,2,16,16,128]{4,3,2,1,0:T(8,128)(2,1)S(1)}, u32[]{:S(2)}, u32[]{:S(2)}) collective-permute-start(bf16[8,2,16,16,128]{4,3,2,1,0:T(8,128)(2,1)S(1)} %bitcast.280), channel_id=1, source_target_pairs={{0,1},{1,0},{2,3},{3,2},{4,5},{5,4},{6,7},{7,6},{8,9},{9,8},{10,11... | collective-permute-start | bytes 3145736 | tf_op jit(solution)/shard_map/ppermute | solution.py:602
  207.3 34.6 %collective-permute-start.2 = (bf16[8,2,16,16,128]{4,3,2,1,0:T(8,128)(2,1)}, bf16[8,2,16,16,128]{4,3,2,1,0:T(8,128)(2,1)}, u32[]{:S(2)}, u32[]{:S(2)}) collective-permute-start(bf16[8,2,16,16,128]{4,3,2,1,0:T(8,128)(2,1)} %collective-permute-done.refs_10_), channel_id=1, source_target_pairs={{0,1},{1,0},{2,3},{3,2},{4,5},{5,4},{6,7},{7,6},{8,9},{9,8},{10,11... | collective-permute-start | bytes 3145736 | tf_op jit(solution)/shard_map/ppermute | solution.py:602
  231.3 39.2 %all-to-all-start.3 = ((bf16[8,2,16,16,128]{4,3,2,1,0:T(8,128)(2,1)}), bf16[8,2,16,16,128]{4,3,2,1,0:T(8,128)(2,1)}, u32[]{:S(2)}, u32[]{:S(2)}) async-start(bf16[8,2,16,16,128]{4,3,2,1,0:T(8,128)(2,1)} %add_convert_fusion.4), calls=%async_computation.3 | async-start | bytes 2097152 | tf_op jit(solution)/shard_map/all_to_all | solution.py:577
  236.9 20.5 %collective-permute-start.21 = (bf16[8,2,16,16,128]{4,3,2,1,0:T(8,128)(2,1)}, bf16[8,2,16,16,128]{4,3,2,1,0:T(8,128)(2,1)}, u32[]{:S(2)}, u32[]{:S(2)}) collective-permute-start(bf16[8,2,16,16,128]{4,3,2,1,0:T(8,128)(2,1)} %get-tuple-element.48), channel_id=1, source_target_pairs={{0,1},{1,0},{2,3},{3,2},{4,5},{5,4},{6,7},{7,6},{8,9},{9,8},{10,11... | collective-permute-start | bytes 3145736 | tf_op jit(solution)/shard_map/ppermute | solution.py:612
  239.7 27.8 %collective-permute-start.23 = (bf16[8,2,16,16,128]{4,3,2,1,0:T(8,128)(2,1)}, bf16[8,2,16,16,128]{4,3,2,1,0:T(8,128)(2,1)}, u32[]{:S(2)}, u32[]{:S(2)}) collective-permute-start(bf16[8,2,16,16,128]{4,3,2,1,0:T(8,128)(2,1)} %add_convert_fusion.1), channel_id=1, source_target_pairs={{2,0},{3,1},{6,4},{7,5},{10,8},{11,9},{14,12},{15,13},{18,16},{19,... | collective-permute-start | bytes 3145736 | tf_op jit(solution)/shard_map/ppermute | solution.py:574
  270.4 33.6 %all-to-all-start.6 = ((bf16[8,2,16,16,128]{4,3,2,1,0:T(8,128)(2,1)}), bf16[8,2,16,16,128]{4,3,2,1,0:T(8,128)(2,1)S(1)}, u32[]{:S(2)}, u32[]{:S(2)}) async-start(bf16[8,2,16,16,128]{4,3,2,1,0:T(8,128)(2,1)} %add_convert_fusion), calls=%async_computation.6 | async-start | bytes 2097152 | tf_op jit(solution)/shard_map/all_to_all | solution.py:577
  277.0 25.6 %collective-permute-start.5 = (bf16[8,2,16,16,128]{4,3,2,1,0:T(8,128)(2,1)S(1)}, bf16[8,2,16,16,128]{4,3,2,1,0:T(8,128)(2,1)S(1)}, u32[]{:S(2)}, u32[]{:S(2)}) collective-permute-start(bf16[8,2,16,16,128]{4,3,2,1,0:T(8,128)(2,1)S(1)} %add_convert_fusion.7), channel_id=1, source_target_pairs={{0,2},{2,0},{1,3},{3,1},{4,6},{6,4},{5,7},{7,5},{8,10},{10,8},{9,1... | collective-permute-start | bytes 3145736 | tf_op jit(solution)/shard_map/ppermute | solution.py:574
  304.0 31.6 %all-to-all-start.1 = ((bf16[8,2,16,16,128]{4,3,2,1,0:T(8,128)(2,1)}), bf16[8,2,16,16,128]{4,3,2,1,0:T(8,128)(2,1)S(1)}, u32[]{:S(2)}, u32[]{:S(2)}) async-start(bf16[8,2,16,16,128]{4,3,2,1,0:T(8,128)(2,1)} %add_convert_fusion.6), calls=%async_computation.1 | async-start | bytes 2097152 | tf_op jit(solution)/shard_map/all_to_all | solution.py:577
  (25 other events, 327.5 us)
